TPU v7x, 256 devices: a whole 4x4x8 slice. The times are simulated.
256 devices in a mesh: head: 8 (over y, core), doc: 32 (over x, z).
Axes of the slice: x: 4, y: 4, z: 8, core: 2. Of those that a mesh axis runs over, the one named last changes fastest.
Arguments:
- tokens: bfloat16 [12288, 1024], P('doc'), may hold values from -6 to 6
- w_qkv: bfloat16 [1024, 3, 1024], P(None, None, 'head'), may hold values from -0.1875 to 0.1875
- w_out: bfloat16 [1024, 1024], P('head'), may hold values from -0.1875 to 0.1875
- w_up: bfloat16 [1024, 4096], P(None, 'head'), may hold values from -0.1875 to 0.1875
- w_down: bfloat16 [4096, 1024], P('head'), may hold values from -0.09375 to 0.09375
- gain_one: float32 [1024], replicated, may hold values from 0.5 to 1.5
- gain_two: float32 [1024], replicated, may hold values from 0.5 to 1.5
- rel_table: bfloat16 [512, 1024], replicated, may hold values from -6 to 6
- prompt_cache: bfloat16 [2, 4096, 1024], P(None, 'doc', 'head'), may hold values from -480 to 480
- w_proj: bfloat16 [1024, 128], replicated, may hold values from -0.1875 to 0.1875
- doc_vectors: bfloat16 [2048, 256, 128], P('doc'), may hold values from -0.5 to 0.5
- doc_lengths: int32 [2048], P('doc'), may hold values from 8 to 256, as said below
- group_ids: int32 [384], P('doc'), may hold values from 0 to 63
- candidates: int32 [384, 64], P('doc', 'head'), may hold values from 0 to 2047, as said below
Outputs:
- query_vectors: bfloat16 [12288, 128], P('doc')
- scores: float32 [384, 64], P('doc', 'head')
Inputs may be any that keep to these rules, and one draw needn't show every extreme that they name: Split candidates into aligned blocks of 12 requests by 8 columns (one index of doc with one of head). Index o of doc holds documents o * 64 to o * 64 + 63. In each block at most 6 entries name documents held by one index of doc, and one index of doc, the same for all blocks, is named by exactly 6 entries of every block. The documents named within one block are distinct. Some document has exactly 256 tokens; token slots from doc_lengths on are padding.
All inputs are finite; a program needn't handle non-finite values.
Results may differ from a plain program's by a relative error of at most 0.02.
Values may be sent and summed in bfloat16 or wider, within the bound.
A program may use at most 128 MiB of HBM per device.

v0:
```python
import math

import jax
import jax.numpy as jnp
from jax import lax
from jax.sharding import PartitionSpec as P

HD = 64
RELS = 512
QLEN = 32
PLEN = 64
DOC_DEV = 64


def layer_norm(values, gain):
    centre = values - jnp.mean(values, axis=-1, keepdims=True)
    spread = jnp.mean(centre * centre, axis=-1, keepdims=True)
    return centre * lax.rsqrt(spread + 1e-07) * gain


def slot_order(holders):
    count = holders.shape[0]
    same = holders[:, None] == holders[None, :]
    earlier = jnp.arange(count)[:, None] > jnp.arange(count)[None, :]
    return jnp.sum(same & earlier, axis=1)


def rate_slots(slot_query, slot_doc, doc_vectors, doc_lengths):
    shape = slot_doc.shape
    flat_doc = slot_doc.reshape(-1)
    flat_query = slot_query.reshape((flat_doc.shape[0],) + slot_query.shape[-2:])
    safe_doc = jnp.maximum(flat_doc, 0)
    documents = doc_vectors[safe_doc]
    lengths = doc_lengths[safe_doc]
    sims = jnp.einsum("sqe,sje->sqj", flat_query, documents, preferred_element_type=jnp.float32)
    live = jnp.arange(documents.shape[1], dtype=jnp.int32)[None, None, :] < lengths[:, None, None]
    best = jnp.max(jnp.where(live, sims, -jnp.inf), axis=2)
    totals = jnp.where(flat_doc >= 0, jnp.sum(best, axis=1), 0.0)
    return totals.reshape(shape)


def body(
    tokens,
    w_qkv,
    w_out,
    w_up,
    w_down,
    gain_one,
    gain_two,
    rel_table,
    prompt_cache,
    w_proj,
    doc_vectors,
    doc_lengths,
    group_ids,
    candidates,
):
    rows_dev = tokens.shape[0]
    req_dev = rows_dev // QLEN
    width = w_qkv.shape[2]
    heads_loc = width // HD
    half = RELS // 2
    scale_root = math.sqrt(3 * HD)
    gathered = lax.all_gather(prompt_cache, "doc", axis=1, tiled=True)
    weights_split = w_qkv.reshape(w_qkv.shape[0], 3, heads_loc, HD)
    projected_all = jnp.einsum(
        "td,dchf->chtf", tokens, weights_split, preferred_element_type=jnp.float32
    ).astype(jnp.bfloat16)
    rel_both = jnp.einsum(
        "rd,dchf->chrf", rel_table, weights_split[:, :2], preferred_element_type=jnp.float32
    ).astype(jnp.bfloat16)
    head_shape = (heads_loc, req_dev, QLEN, HD)
    query_four = projected_all[0].reshape(head_shape)
    keys_four = projected_all[1].reshape(head_shape)
    values_four = projected_all[2].reshape(head_shape)
    groups_all = gathered.shape[1] // PLEN
    cache_all = gathered.reshape(2, groups_all, PLEN, heads_loc, HD)
    picked = jnp.transpose(cache_all[:, group_ids], (0, 3, 1, 2, 4))
    keys = jnp.concatenate([keys_four, picked[0]], axis=2)
    values = jnp.concatenate([values_four, picked[1]], axis=2)
    pos_query = PLEN + jnp.arange(QLEN, dtype=jnp.int32)
    pos_key = jnp.concatenate([pos_query, jnp.arange(PLEN, dtype=jnp.int32)])
    index_one = pos_query[:, None] - pos_key[None, :] + half
    index_two = pos_key[:, None] - pos_query[None, :] + half
    rel_k_rows = rel_both[1][:, index_one]
    rel_q_rows = rel_both[0][:, index_two]
    c2p = jnp.einsum("hrqd,hqkd->hrqk", query_four, rel_k_rows, preferred_element_type=jnp.float32)
    p2c = jnp.einsum("hrkd,hkqd->hrqk", keys, rel_q_rows, preferred_element_type=jnp.float32)
    content = jnp.einsum("hrqd,hrkd->hrqk", query_four, keys, preferred_element_type=jnp.float32)
    logits = (content + c2p + p2c) / scale_root
    largest = jnp.max(logits, axis=-1, keepdims=True)
    weights = jnp.exp(logits - largest)
    denominator = jnp.sum(weights, axis=-1)
    summed = jnp.einsum(
        "hrqk,hrkd->hrqd", weights.astype(jnp.bfloat16), values, preferred_element_type=jnp.float32
    )
    attended = (summed / denominator[..., None]).astype(jnp.bfloat16)
    out_split = w_out.reshape(heads_loc, HD, w_out.shape[1])
    attn_part = jnp.einsum(
        "hrqd,hde->rqe", attended, out_split, preferred_element_type=jnp.float32
    ).reshape(rows_dev, w_out.shape[1])
    attn_total = lax.psum(attn_part.astype(jnp.bfloat16), "head").astype(jnp.float32)
    hidden_one = layer_norm(tokens.astype(jnp.float32) + attn_total, gain_one).astype(jnp.bfloat16)
    inner = jax.nn.gelu(
        jnp.dot(hidden_one, w_up, preferred_element_type=jnp.float32), approximate=False
    ).astype(jnp.bfloat16)
    ffn_total = lax.psum(
        jnp.dot(inner, w_down, preferred_element_type=jnp.float32).astype(jnp.bfloat16), "head"
    ).astype(jnp.float32)
    hidden_two = layer_norm(hidden_one.astype(jnp.float32) + ffn_total, gain_two).astype(
        jnp.bfloat16
    )
    projected = jnp.dot(hidden_two, w_proj, preferred_element_type=jnp.float32)
    query_vectors = (
        projected * lax.rsqrt(jnp.sum(projected * projected, axis=-1, keepdims=True) + 1e-06)
    ).astype(jnp.bfloat16)
    shards = lax.axis_size("doc")
    cand_dev = candidates.shape[1]
    pairs = req_dev * cand_dev
    capacity = max(2, 2 * pairs // shards)
    flat_cand = candidates.reshape(-1)
    holders = flat_cand // DOC_DEV
    request_of = jnp.arange(pairs, dtype=jnp.int32) // cand_dev
    slot_rank = slot_order(holders)
    copies, cand_copies = (
        lax.all_gather(query_vectors, "doc", axis=0, tiled=True),
        lax.all_gather(candidates, "doc", axis=0, tiled=True),
    )
    all_query = copies.reshape(shards, req_dev, QLEN, copies.shape[1])
    all_cand = cand_copies.reshape(shards, pairs)
    holder_all = all_cand // DOC_DEV
    local_all = all_cand % DOC_DEV
    rank_all = jax.vmap(slot_order)(holder_all)
    own_index = lax.axis_index("doc")
    chosen = (holder_all[:, None, :] == own_index) & (
        rank_all[:, None, :] == jnp.arange(capacity, dtype=jnp.int32)[None, :, None]
    )
    filled = jnp.any(chosen, axis=2)
    slot_request = jnp.sum(jnp.where(chosen, request_of[None, None, :], 0), axis=2)
    slot_doc = jnp.where(
        filled, jnp.sum(jnp.where(chosen, local_all[:, None, :], 0), axis=2), -1
    ).astype(jnp.int32)
    slot_query = all_query[jnp.arange(shards)[:, None], slot_request]
    slot_scores = rate_slots(slot_query, slot_doc, doc_vectors, doc_lengths)
    returned = lax.all_to_all(slot_scores, "doc", split_axis=0, concat_axis=0, tiled=True)
    scores = returned.reshape(-1)[holders * capacity + slot_rank].reshape(candidates.shape)
    return (query_vectors, scores)


def solution(mesh):
    placed = (
        P("doc", None),
        P(None, None, "head"),
        P("head", None),
        P(None, "head"),
        P("head", None),
        P(),
        P(),
        P(),
        P(None, "doc", "head"),
        P(),
        P("doc", None, None),
        P("doc"),
        P("doc"),
        P("doc", "head"),
    )
    return jax.shard_map(
        body,
        mesh=mesh,
        in_specs=placed,
        out_specs=(P("doc", None), P("doc", "head")),
        check_vma=False,
    )
```

profile of v0, /device:TPU:1, one launch (start us, length us, event | category | flops | bytes accessed | tf_op | source)
XLA Modules:
  0.0 381.4 jit_solution(13940295378734445451)
XLA Ops:
  10.3 20.3 %gather_fusion.2 = bf16[3072,2,64]{2,1,0:T(2,128)(2,1)} fusion(bf16[2,512,64]{2,0,1:T(2,128)(2,1)S(1)} %copy.193, s32[3072]{0:T(1024)S(1)} %broadcast_clamp_fusion), kind=kCustom, calls=%fused_computation.2 | custom fusion | bytes 1585152 | tf_op jit(solution)/shard_map/gather | solution.py:86
  30.6 2.9 copy.194
  35.6 20.3 %gather_fusion.1 = bf16[3072,2,64]{2,1,0:T(2,128)(2,1)} fusion(bf16[2,512,64]{2,0,1:T(2,128)(2,1)S(1)} %copy.189, s32[3072]{0:T(1024)S(1)} %broadcast_clamp_fusion.1), kind=kCustom, calls=%fused_computation.1 | custom fusion | bytes 1585152 | tf_op jit(solution)/shard_map/gather | solution.py:85
  55.9 4.0 %copy.190 = bf16[32,96,2,64]{1,3,0,2:T(8,128)(2,1)S(1)} copy(bf16[32,96,2,64]{3,2,1,0:T(2,128)(2,1)} %bitcast.83) | data formatting | bytes 1572864 | tf_op jit(solution)/shard_map/gather | solution.py:85
  61.0 1.7 copy.197
  62.7 1.9 copy.198
  65.7 22.7 %all-gather.4.cloned.1.call-done = bf16[2,4096,128]{2,1,0:T(8,128)(2,1)} async-done(((bf16[2,128,128]{2,1,0:T(8,128)(2,1)}), bf16[2,4096,128]{2,1,0:T(8,128)(2,1)}) %all-gather.4.cloned.1.call-update) | async-done | bytes 2097168 | tf_op jit(solution)/shard_map/all_gather | solution.py:64
  88.4 8.2 %reshape.599 = bf16[2,64,64,2,64]{4,3,2,1,0:T(2,128)(2,1)} reshape(bf16[2,4096,128]{2,1,0:T(8,128)(2,1)} %all-gather.4.cloned.1.call-done) | data formatting | bytes 4194304 | tf_op jit(solution)/shard_map/reshape | solution.py:77
  96.7 5.4 %copy.186 = bf16[2,64,64,2,64]{4,2,3,1,0:T(8,128)(2,1)} copy(bf16[2,64,64,2,64]{4,3,2,1,0:T(2,128)(2,1)} %reshape.599) | data formatting | bytes 4194304 | tf_op jit(solution)/shard_map/reshape | solution.py:77
  102.1 3.7 gather_fusion
  109.0 3.5 fusion.107
  112.5 1.9 copy.196
  117.5 65.8 %all-reduce.3.cloned.1.call-done = bf16[384,1024]{1,0:T(8,128)(2,1)} async-done(((bf16[384,1024]{1,0:T(8,128)(2,1)}), bf16[384,1024]{1,0:T(8,128)(2,1)}) %all-reduce.3.cloned.1.call-update) | async-done | bytes 786448 | tf_op jit(solution)/shard_map/psum | solution.py:102
  185.6 4.8 %convolution_convert_fusion = bf16[384,1024]{1,0:T(8,128)(2,1)} fusion(bf16[512,1024]{1,0:T(8,128)(2,1)S(1)} %copy-done, bf16[384,1024]{1,0:T(8,128)(2,1)S(1)} %multiply_convert_fusion.1, bf16[1024,512]{1,0:T(8,128)(2,1)} %param.17), kind=kOutput, calls=%fused_computation.20 | convolution fusion | flops 818479104 | bytes 3670016 | tf_op jit(solution)/shard_map/dot_general | solution.py:108
  190.5 66.1 %all-reduce.5.cloned.1.call-done = bf16[384,1024]{1,0:T(8,128)(2,1)} async-done(((bf16[384,1024]{1,0:T(8,128)(2,1)}), bf16[384,1024]{1,0:T(8,128)(2,1)}) %all-reduce.5.cloned.1.call-update) | async-done | bytes 786448 | tf_op jit(solution)/shard_map/psum | solution.py:107
  260.1 35.6 %all-gather = s32[32,12,8]{1,2,0:T(8,128)S(1)} all-gather(s32[1,12,8]{1,2,0:T(8,128)S(1)} %bitcast.95), channel_id=1, replica_groups=mesh['head'=8,'doc'=32] {'doc'}, dimensions={0}, use_global_device_ids=true | all-gather | bytes 12672 | tf_op jit(solution)/shard_map/all_gather | solution.py:127
  298.1 10.3 %gather_fusion.5 = bf16[192,256,128]{2,1,0:T(8,128)(2,1)} fusion(bf16[64,256,128]{2,1,0:T(8,128)(2,1)} %param.24, s32[1024]{0:T(1024)S(1)} %pad_clamp_fusion.1), kind=kCustom, calls=%fused_computation.5 | custom fusion | bytes 25166592 | tf_op jit(solution)/shard_map/gather | solution.py:33
  308.4 1.5 gather_fusion.3
  310.3 27.3 %all-gather.6.cloned.1.call-done = bf16[12288,128]{0,1:T(8,128)(2,1)} async-done(((bf16[384,128]{0,1:T(8,128)(2,1)}), bf16[12288,128]{0,1:T(8,128)(2,1)}) %all-gather.6.cloned.1.call-update) | async-done | bytes 3145744 | tf_op jit(solution)/shard_map/all_gather | solution.py:126
  337.6 4.7 %copy.206 = bf16[12288,128]{1,0:T(8,128)(2,1)} copy(bf16[12288,128]{0,1:T(8,128)(2,1)} %all-gather.6.cloned.1.call-done) | data formatting | bytes 6291456 | tf_op jit(solution)/shard_map/all_gather | solution.py:126
  342.3 3.7 gather_fusion.4
  346.0 9.2 %select_reduce_fusion = f32[192,32]{1,0:T(8,128)S(1)} fusion(pred[192,256]{1,0:T(8,128)(4,1)S(1)} %iota_compare_fusion, bf16[192,32,128]{2,1,0:T(8,128)(2,1)S(1)} %gather_fusion.4, bf16[192,256,128]{2,1,0:T(8,128)(2,1)} %gather_fusion.5), kind=kOutput, calls=%fused_computation.7 | convolution fusion | flops 405792768 | bytes 14229504 | tf_op jit(solution)/shard_map/sqe,sje->sqj/dot_general | solution.py:35
  356.2 6.7 %all-to-all-start = ((f32[32,1,6]{2,1,0:T(1,128)}), f32[32,1,6]{2,1,0:T(1,128)S(1)}, u32[]{:S(2)}, u32[]{:S(2)}) async-start(f32[32,1,6]{2,1,0:T(1,128)} %copy.210), calls=%async_computation | async-start | bytes 32768 | tf_op jit(solution)/shard_map/all_to_all | solution.py:145
  363.7 7.8 %all-to-all-done = f32[32,1,6]{2,1,0:T(1,128)S(1)} async-done(((f32[32,1,6]{2,1,0:T(1,128)}), f32[32,1,6]{2,1,0:T(1,128)S(1)}, u32[]{:S(2)}, u32[]{:S(2)}) %all-to-all-start) | async-done | bytes 800 | tf_op jit(solution)/shard_map/all_to_all | solution.py:145
  (118 shorter events, 27.0 us)
Async XLA Ops:
  7.2 178.4 %copy-start = (bf16[512,1024]{1,0:T(8,128)(2,1)S(1)}, bf16[512,1024]{1,0:T(8,128)(2,1)}, u32[]{:S(2)}) copy-start(bf16[512,1024]{1,0:T(8,128)(2,1)} %param.18) | copy-start | bytes 3145732
  7.2 2.5 copy-start.6
  7.2 81.3 %all-gather.4.cloned.1.call-start = ((), (), s32[]{:S(2)}) async-start(), calls=%async_computation.1 | async-start | bytes 2162688 | tf_op jit(solution)/shard_map/all_gather | solution.py:64
  7.9 175.4 %all-reduce.3.cloned.1.call-start = ((), (), s32[]{:S(2)}) async-start(), calls=%async_computation.2 | async-start | bytes 1572864 | tf_op jit(solution)/shard_map/psum | solution.py:102
  30.6 2.9 copy-start.2
  55.9 8.7 %copy-start.15 = (s32[12]{0:T(128)S(1)}, s32[12]{0:T(128)}, u32[]{:S(2)}) copy-start(s32[12]{0:T(128)} %param.26) | copy-start | bytes 148
  112.5 1.9 copy-start.5
  114.4 1.0 copy-start.8
  114.4 1.1 copy-start.9
  114.8 1.2 copy-start.10
  117.3 68.0 %copy-start.12 = (f32[1024]{0:T(1024)S(1)}, f32[1024]{0:T(1024)}, u32[]{:S(2)}) copy-start(f32[1024]{0:T(1024)} %param.19) | copy-start | bytes 12292
  117.3 139.3 %all-reduce.5.cloned.1.call-start = ((), (), s32[]{:S(2)}) async-start(), calls=%async_computation.3 | async-start | bytes 1572864 | tf_op jit(solution)/shard_map/psum | solution.py:107
  183.3 1.5 copy-start.3
  190.5 68.1 %copy-start.13 = (bf16[1024,128]{1,0:T(8,128)(2,1)S(1)}, bf16[1024,128]{1,0:T(8,128)(2,1)}, u32[]{:S(2)}) copy-start(bf16[1024,128]{1,0:T(8,128)(2,1)} %param.23) | copy-start | bytes 786436
  190.5 68.1 %copy-start.14 = (f32[1024]{0:T(1024)S(1)}, f32[1024]{0:T(1024)}, u32[]{:S(2)}) copy-start(f32[1024]{0:T(1024)} %param.20) | copy-start | bytes 12292
  190.5 147.1 %all-gather.6.cloned.1.call-start = ((), (), s32[]{:S(2)}) async-start(), calls=%async_computation.4 | async-start | bytes 3244032 | tf_op jit(solution)/shard_map/all_gather | solution.py:126
  256.6 1.5 copy-start.4
  258.6 1.3 copy-start.11
  298.1 10.3 %copy-start.1 = (s32[64]{0:T(128)S(1)}, s32[64]{0:T(128)}, u32[]{:S(2)}) copy-start(s32[64]{0:T(128)} %param.25) | copy-start | bytes 772
  346.0 16.9 %copy-start.7 = (bf16[384,128]{0,1:T(8,128)(2,1)S(1)}, bf16[384,128]{0,1:T(8,128)(2,1)}, u32[]{:S(2)}) copy-start(bf16[384,128]{0,1:T(8,128)(2,1)} %multiply_convert_fusion.3) | copy-start | bytes 294916
  356.2 15.4 %all-to-all-start = ((f32[32,1,6]{2,1,0:T(1,128)}), f32[32,1,6]{2,1,0:T(1,128)S(1)}, u32[]{:S(2)}, u32[]{:S(2)}) async-start(f32[32,1,6]{2,1,0:T(1,128)} %copy.210), calls=%async_computation | async-start | bytes 32768 | tf_op jit(solution)/shard_map/all_to_all | solution.py:145
Sparse Core Ops, SparseCore 0:
  10.6 77.7 all-gather.3
  117.4 65.8 all-reduce.2
  190.6 66.0 all-reduce.4
  260.0 77.5 all-gather.5
where the time goes:
time: 387 us; the launch traced here: 381 us
  waiting for transfers between devices  190 us (49%)
  local copies, waits for them, and re-layouts  103 us (27%)
  blocking collectives  35.6 us (9%)
  matrix products  22.4 us (6%)
  between operations  14.2 us (4%)
  other arithmetic  8.49 us (2%)
  starting transfers between devices  7.07 us (2%)
    psum x1, waiting for transfers between devices, body(): lax.psum(jnp.dot(inner, w_down, preferred_element_type=jnp.float32).astyp...  66.1 us
    psum x1, waiting for transfers between devices, body(): lax.psum(attn_part.astype(jnp.bfloat16), 'head').astype(jnp.float32)  65.8 us
    all_gather x1, blocking collectives, body(): lax.all_gather(candidates, 'doc', axis=0, tiled=True)  35.6 us
    all_gather x1, waiting for transfers between devices, body(): lax.all_gather(query_vectors, 'doc', axis=0, tiled=True)  27.3 us
    gather x2, local copies, waits for them, and re-layouts, body(): rel_k_rows = rel_both[1][:, index_one]  24.3 us
    gather x2, local copies, waits for them, and re-layouts, body(): rel_q_rows = rel_both[0][:, index_two]  23.2 us
    all_gather x1, waiting for transfers between devices, body(): gathered = lax.all_gather(prompt_cache, 'doc', axis=1, tiled=True)  22.7 us
    reshape x2, local copies, waits for them, and re-layouts, body(): cache_all = gathered.reshape(2, groups_all, PLEN, heads_loc, HD)  13.7 us
  transfers between devices with their start and end apart: 5, of which 5 were waited for; matrix products, arithmetic and copies ran while one was open for 19% of the time, Pallas kernels for 0%

commit v1 on v0

v1 whole, which is shorter than its diff:
```python
import functools
import math

import jax
import jax.numpy as jnp
from jax import lax
from jax.experimental import pallas as pl
from jax.experimental.pallas import tpu as pltpu
from jax.sharding import PartitionSpec as P

HD = 64
RELS = 512
QLEN = 32
PLEN = 64
DOC_DEV = 64
NX = 4
NZ = 8
NY = 4
MESH = pl.DeviceIdType.MESH
F32 = jnp.float32
BF16 = jnp.bfloat16
NT = (((1,), (1,)), ((), ()))


def mod(value, size):
    return lax.rem(value + 4 * size, size)


class Message:
    def __init__(self, kv, axis, sign, dx, dz, low, rows, parent):
        self.kv, self.axis, self.sign, self.dx, self.dz = kv, axis, sign, dx, dz
        self.low, self.rows, self.parent = low, rows, parent
        self.children = []
        self.time = None
        self.index = None


def plan_gather():
    made = []

    def add(kv, axis, sign, dx, dz, low, rows, parent):
        message = Message(kv, axis, sign, dx, dz, low, rows, parent)
        made.append(message)
        return message

    def along_x(kv, dz, low, rows, parent):
        out = []
        for sign in (1, -1):
            near = add(kv, "x", sign, sign, dz, low, rows, parent)
            half = rows // 2
            far = add(kv, "x", sign, 2 * sign, dz, low if sign > 0 else low + half, half, near)
            out += [near, far]
        return out

    def along_z(kv, dx, low, rows, parent):
        out = []
        for sign in (1, -1):
            previous = parent
            for step in range(1, 4):
                previous = add(kv, "z", sign, dx, sign * step, low, rows, previous)
                out.append(previous)
            half = rows // 2
            out.append(add(kv, "z", sign, dx, sign * 4, low if sign > 0 else low + half, half, previous))
        return out

    firsts = along_z(0, 0, 0, 128, None)
    along_x(0, 0, 0, 128, None)
    for first in firsts:
        along_x(0, first.dz, first.low, first.rows, first)
    firsts = along_x(1, 0, 0, 128, None)
    along_z(1, 0, 0, 128, None)
    for first in firsts:
        along_z(1, first.dx, first.low, first.rows, first)
    for message in made:
        if message.parent is not None:
            message.parent.children.append(message)
    free = {}
    ready = [(0.0, i) for i, m in enumerate(made) if m.parent is None]
    while ready:
        ready.sort()
        start, i = ready.pop(0)
        message = made[i]
        link = (message.axis, message.sign)
        begin = max(start, free.get(link, 0.0))
        free[link] = begin + message.rows * 256 / 46500.0
        message.time = free[link] + 1.6
        ready += [(message.time, made.index(child)) for child in message.children]
    order = sorted(made, key=lambda m: m.time)
    for index, message in enumerate(order):
        message.index = index
    return order


def norm_rows(values, gain):
    centre = values - jnp.mean(values, axis=-1, keepdims=True)
    spread = jnp.mean(centre * centre, axis=-1, keepdims=True)
    return centre * lax.rsqrt(spread + 1e-07) * gain


def gelu(values):
    return 0.5 * values * (1.0 + lax.erf(values * (1.0 / math.sqrt(2.0))))


def encoder_kernel(
    plan,
    group_ref,
    tokens_hbm,
    w_qkv_hbm,
    w_out_hbm,
    w_up_hbm,
    w_down_hbm,
    gain_one_ref,
    gain_two_ref,
    rel_hbm,
    cache_hbm,
    w_proj_ref,
    query_out,
    cache,
    tokens,
    w_qkv,
    w_out,
    w_up,
    w_down,
    rel,
    q_mask,
    k_own,
    v_own,
    q_rel,
    rel_two,
    att,
    att_send,
    opp_send,
    side_send,
    opp_recv,
    side_recv,
    hidden,
    vectors,
    load_sem,
    gather_send,
    gather_recv,
    swap_send,
    swap_recv,
    att_sem,
    opp_send_sem,
    opp_recv_sem,
    side_send_sem,
    side_recv_sem,
    hid_send_sem,
    hid_recv_sem,
    vec_send_sem,
    vec_recv_sem,
):
    head = lax.axis_index("head")
    doc = lax.axis_index("doc")
    y, core = lax.div(head, 2), lax.rem(head, 2)
    x, z = lax.div(doc, NZ), lax.rem(doc, NZ)
    partner = (2 * y + 1 - core, doc)
    y_up, y_down = mod(y + 1, NY), mod(y - 1, NY)
    y_far = mod(y + 2, NY)

    def at_y(other):
        return (2 * other + core, doc)

    def at_link(axis, sign):
        if axis == "x":
            return (head, mod(x + sign, NX) * NZ + z)
        return (head, x * NZ + mod(z + sign, NZ))

    peers = [partner]
    for other in (y_up, y_down, y_far):
        peers += [(2 * other + core, doc), (2 * other + 1 - core, doc)]
    links = [at_link(axis, sign) for axis in ("x", "z") for sign in (1, -1)]
    barrier = pltpu.get_barrier_semaphore()
    for device in peers + links:
        pl.semaphore_signal(barrier, inc=1, device_id=device, device_id_type=MESH)

    loads = [
        pltpu.make_async_copy(tokens_hbm, tokens, load_sem.at[0]),
        pltpu.make_async_copy(w_qkv_hbm, w_qkv, load_sem.at[1]),
        pltpu.make_async_copy(rel_hbm.at[pl.ds(RELS // 2 - 96, 128)], rel.at[0], load_sem.at[2]),
        pltpu.make_async_copy(rel_hbm.at[pl.ds(RELS // 2 - 32, 128)], rel.at[1], load_sem.at[3]),
        pltpu.make_async_copy(
            cache_hbm, cache.at[:, pl.ds(doc * 2, 2)], load_sem.at[4]
        ),
        pltpu.make_async_copy(w_out_hbm, w_out.at[core], load_sem.at[5]),
        pltpu.make_async_copy(w_up_hbm, w_up.at[core], load_sem.at[6]),
        pltpu.make_async_copy(w_down_hbm, w_down.at[core], load_sem.at[7]),
    ]
    for load in loads:
        load.start()
    pl.semaphore_wait(barrier, len(peers) + len(links))

    def gather_copy(message):
        dx, dz = message.dx, message.dz
        if message.axis == "x":
            dx -= message.sign
        else:
            dz -= message.sign
        block = mod(x - dx, NX) * NZ + mod(z - dz, NZ)
        group, low = block * 2 + message.low // PLEN, message.low % PLEN
        if message.rows == 2 * PLEN:
            target = cache.at[message.kv, pl.ds(group, 2)]
        else:
            target = cache.at[message.kv, group, pl.ds(low, message.rows)]
        source = cache_hbm.at[message.kv] if message.parent is None else target
        return pltpu.make_async_remote_copy(
            src_ref=source,
            dst_ref=target,
            send_sem=gather_send.at[message.index],
            recv_sem=gather_recv.at[message.index],
            device_id=at_link(message.axis, message.sign),
            device_id_type=MESH,
        )

    copies = {message.index: gather_copy(message) for message in plan}
    for message in plan:
        if message.parent is None:
            copies[message.index].start()

    swaps = []
    for i, (source, target) in enumerate(((w_out_hbm, w_out), (w_up_hbm, w_up), (w_down_hbm, w_down))):
        swaps.append(
            pltpu.make_async_remote_copy(
                src_ref=source,
                dst_ref=target.at[core],
                send_sem=swap_send.at[i],
                recv_sem=swap_recv.at[i],
                device_id=partner,
                device_id_type=MESH,
            )
        )
        swaps[-1].start()

    loads[0].wait()
    loads[1].wait()
    low_head = lax.broadcasted_iota(jnp.int32, (128, 128), 1) < HD
    for block in range(3):
        rows = slice(block * 128, block * 128 + 128)
        made = jnp.dot(tokens[rows, :], w_qkv[...], preferred_element_type=F32)
        q_made = made[:, :128]
        q_mask[0, rows, :] = jnp.where(low_head, q_made, 0.0).astype(BF16)
        q_mask[1, rows, :] = jnp.where(low_head, 0.0, q_made).astype(BF16)
        k_own[rows, :] = made[:, 128:256].astype(BF16)
        v_own[rows, :] = made[:, 256:].astype(BF16)
    loads[2].wait()
    loads[3].wait()
    flip = (
        lax.broadcasted_iota(jnp.int32, (128, 128), 0) + lax.broadcasted_iota(jnp.int32, (128, 128), 1)
        == 127
    ).astype(F32).astype(BF16)
    for i in range(2):
        row = jnp.dot(
            rel[i], w_qkv[:, i * 128 : i * 128 + 128], preferred_element_type=F32
        ).astype(BF16)
        turned = jnp.dot(flip, row, preferred_element_type=F32)
        rel_two[i, 0:128, :] = jnp.where(low_head, turned, 0.0).astype(BF16)
        rel_two[i, 128:256, :] = jnp.where(low_head, 0.0, turned).astype(BF16)
    for block in range(3):
        rows = slice(block * 128, block * 128 + 128)
        q_all = q_mask[0, rows, :] + q_mask[1, rows, :]
        q_rel[rows, :] = lax.dot_general(q_all, rel_two[1], NT, preferred_element_type=F32)
    loads[4].wait()

    for message in plan:
        copies[message.index].wait_recv()
        for child in message.children:
            copies[child.index].start()

    low_lane = lax.broadcasted_iota(jnp.int32, (96, 128), 1) < QLEN
    low_half = lax.broadcasted_iota(jnp.int32, (QLEN, 128), 1) < HD

    def attend(request):
        group = group_ref[request]
        own = pl.ds(pl.multiple_of(request * QLEN, QLEN), QLEN)
        keys = jnp.concatenate([cache[0, group], k_own[own, :]], axis=0)
        values = jnp.concatenate([cache[1, group], v_own[own, :]], axis=0)
        query = jnp.concatenate([q_mask[0, own, :], q_mask[1, own, :]], axis=0)
        content = lax.dot_general(query, keys, NT, preferred_element_type=F32)
        key_rel = lax.dot_general(keys, rel_two[0], NT, preferred_element_type=F32)
        first = pltpu.roll(key_rel[:, :128], 33, 1, stride=1, stride_axis=0)
        second = pltpu.roll(key_rel[:, 128:], 65, 1, stride=1, stride_axis=0)
        p2c = jnp.transpose(jnp.where(low_lane, first, second))[: 2 * QLEN, :]
        mine = q_rel[own, :]
        c2p = jnp.concatenate(
            [
                pltpu.roll(mine[:, :128], 97, 1, stride=1, stride_axis=0),
                pltpu.roll(mine[:, 128:], 97, 1, stride=1, stride_axis=0),
            ],
            axis=0,
        )[:, :96]
        logits = (content + c2p + p2c) * (1.0 / math.sqrt(3 * HD))
        weights = jnp.exp(logits - jnp.max(logits, axis=-1, keepdims=True))
        total = jnp.sum(weights, axis=-1, keepdims=True)
        out = jnp.dot(weights.astype(BF16), values, preferred_element_type=F32) / total
        return jnp.where(low_half, out[:QLEN], out[QLEN:]).astype(BF16)

    half = tokens.shape[0] // 2
    per_core = half // QLEN
    for i in range(per_core):
        att_send[i * QLEN : i * QLEN + QLEN, :] = attend((1 - core) * per_core + i)
    att_copy = pltpu.make_async_remote_copy(
        src_ref=att_send,
        dst_ref=att.at[core],
        send_sem=att_sem.at[0],
        recv_sem=att_sem.at[1],
        device_id=partner,
        device_id_type=MESH,
    )
    att_copy.start()
    for i in range(per_core):
        att[core, i * QLEN : i * QLEN + QLEN, :] = attend(core * per_core + i)
    att_copy.wait_recv()
    loads[5].wait()
    swaps[0].wait_recv()
    part = half // NY

    def chunk_rows(other):
        return pl.ds(pl.multiple_of(other * part, 16), part)

    def out_part(other):
        rows = chunk_rows(other)
        return jnp.dot(att[0, rows, :], w_out[0], preferred_element_type=F32) + jnp.dot(
            att[1, rows, :], w_out[1], preferred_element_type=F32
        )

    def side_copy(phase, side, piece):
        return pltpu.make_async_remote_copy(
            src_ref=side_send.at[phase, side, piece],
            dst_ref=side_recv.at[phase, side, piece],
            send_sem=side_send_sem.at[phase, side, piece],
            recv_sem=side_recv_sem.at[phase, side, piece],
            device_id=at_y(y_down if side else y_up),
            device_id_type=MESH,
        )

    def far_copy(phase, piece):
        return pltpu.make_async_remote_copy(
            src_ref=opp_send.at[phase, piece],
            dst_ref=opp_recv.at[phase, piece],
            send_sem=opp_send_sem.at[phase, piece],
            recv_sem=opp_recv_sem.at[phase, piece],
            device_id=at_y(y_down if piece else y_up),
            device_id_type=MESH,
        )

    wide = 512

    def reduce_rows(phase, far, up, down, own):
        sent = []
        share = far()
        for piece in range(2):
            opp_send[phase, piece] = share[:, piece * wide : piece * wide + wide].astype(BF16)
            copy = far_copy(phase, piece)
            copy.start()
            sent.append(copy)
        share_up, share_down = up(), down()
        side_send[phase, 0, 1] = share_up[:, wide:].astype(BF16)
        side_send[phase, 1, 0] = share_down[:, :wide].astype(BF16)
        for side, piece in ((0, 1), (1, 0)):
            copy = side_copy(phase, side, piece)
            copy.start()
            sent.append(copy)
        share_own = own()
        far_copy(phase, 0).wait_recv()
        side_send[phase, 0, 0] = (share_up[:, :wide] + opp_recv[phase, 0].astype(F32)).astype(BF16)
        copy = side_copy(phase, 0, 0)
        copy.start()
        sent.append(copy)
        far_copy(phase, 1).wait_recv()
        side_send[phase, 1, 1] = (share_down[:, wide:] + opp_recv[phase, 1].astype(F32)).astype(BF16)
        copy = side_copy(phase, 1, 1)
        copy.start()
        sent.append(copy)
        for side, piece in ((0, 1), (1, 0), (0, 0), (1, 1)):
            side_copy(phase, side, piece).wait_recv()
        halves = [
            share_own[:, piece * wide : piece * wide + wide]
            + side_recv[phase, 0, piece].astype(F32)
            + side_recv[phase, 1, piece].astype(F32)
            for piece in range(2)
        ]
        return jnp.concatenate(halves, axis=1), sent

    total, sent_one = reduce_rows(
        0,
        lambda: out_part(y_far),
        lambda: out_part(y_up),
        lambda: out_part(y_down),
        lambda: out_part(y),
    )
    own_rows = pl.ds(pl.multiple_of(core * half + y * part, 16), part)
    one = norm_rows(tokens[own_rows, :].astype(F32) + total, gain_one_ref[...]).astype(BF16)
    for piece in range(2):
        hidden[y, piece] = one[:, piece * wide : piece * wide + wide]

    def hidden_copy(side, hop, piece):
        block = y if hop == 0 else (y_up if side else y_down)
        return pltpu.make_async_remote_copy(
            src_ref=hidden.at[block, piece],
            dst_ref=hidden.at[block, piece],
            send_sem=hid_send_sem.at[side, hop, piece],
            recv_sem=hid_recv_sem.at[side, hop, piece],
            device_id=at_y(y_down if side else y_up),
            device_id_type=MESH,
        )

    sent_two = []

    def send_hidden(side, hop, piece):
        copy = hidden_copy(side, hop, piece)
        copy.start()
        sent_two.append(copy)

    send_hidden(0, 0, 0)
    send_hidden(1, 0, 1)
    send_hidden(0, 0, 1)
    send_hidden(1, 0, 0)
    for i in (6, 7):
        loads[i].wait()
    swaps[1].wait_recv()
    swaps[2].wait_recv()

    def feed(other):
        rows = jnp.concatenate([hidden[other, 0], hidden[other, 1]], axis=1)
        made = None
        for i in range(2):
            inner = gelu(jnp.dot(rows, w_up[i], preferred_element_type=F32)).astype(BF16)
            term = jnp.dot(inner, w_down[i], preferred_element_type=F32)
            made = term if made is None else made + term
        return made

    feed_own = feed(y)
    hidden_copy(0, 0, 0).wait_recv()
    send_hidden(0, 1, 0)
    hidden_copy(1, 0, 1).wait_recv()
    send_hidden(1, 1, 1)
    hidden_copy(0, 0, 1).wait_recv()
    hidden_copy(1, 0, 0).wait_recv()
    feed_up, feed_down = feed(y_up), feed(y_down)
    hidden_copy(0, 1, 0).wait_recv()
    hidden_copy(1, 1, 1).wait_recv()
    total_two, sent_three = reduce_rows(
        1, lambda: feed(y_far), lambda: feed_up, lambda: feed_down, lambda: feed_own
    )
    two = norm_rows(one.astype(F32) + total_two, gain_two_ref[...]).astype(BF16)
    projected = jnp.dot(two, w_proj_ref[...], preferred_element_type=F32)
    unit = projected * lax.rsqrt(jnp.sum(projected * projected, axis=-1, keepdims=True) + 1e-06)
    vectors[head] = unit.astype(BF16)

    sent_four = []
    for i, device in enumerate(peers):
        copy = pltpu.make_async_remote_copy(
            src_ref=vectors.at[head],
            dst_ref=vectors.at[head],
            send_sem=vec_send_sem.at[i],
            recv_sem=vec_recv_sem.at[i],
            device_id=device,
            device_id_type=MESH,
        )
        copy.start()
        sent_four.append(copy)
    for copy in sent_four:
        copy.wait_recv()
    for block in range(2 * NY):
        place = (block % 2) * half + (block // 2) * part
        query_out[place : place + part, :] = vectors[block]

    for copy in list(copies.values()) + swaps + [att_copy] + sent_one + sent_two + sent_three + sent_four:
        copy.wait_send()


def encode(tokens, w_qkv, w_out, w_up, w_down, gain_one, gain_two, rel_table, prompt_cache, w_proj, group_ids):
    plan = plan_gather()
    rows, width = tokens.shape
    half = rows // 2
    part = half // NY
    anywhere = pl.BlockSpec(memory_space=pl.ANY)
    vmem = pl.BlockSpec(memory_space=pltpu.VMEM)
    smem = pl.BlockSpec(memory_space=pltpu.SMEM)
    dma = pltpu.SemaphoreType.DMA
    return pl.pallas_call(
        functools.partial(encoder_kernel, plan),
        out_shape=jax.ShapeDtypeStruct((rows, 128), BF16),
        in_specs=[smem] + [anywhere] * 5 + [vmem, vmem, anywhere, anywhere, vmem],
        out_specs=vmem,
        scratch_shapes=[
            pltpu.VMEM((2, 64, PLEN, 128), BF16),
            pltpu.VMEM((rows, width), BF16),
            pltpu.VMEM((width, 384), BF16),
            pltpu.VMEM((2, 128, width), BF16),
            pltpu.VMEM((2, width, 512), BF16),
            pltpu.VMEM((2, 512, width), BF16),
            pltpu.VMEM((2, 128, width), BF16),
            pltpu.VMEM((2, rows, 128), BF16),
            pltpu.VMEM((rows, 128), BF16),
            pltpu.VMEM((rows, 128), BF16),
            pltpu.VMEM((rows, 256), F32),
            pltpu.VMEM((2, 256, 128), BF16),
            pltpu.VMEM((2, half, 128), BF16),
            pltpu.VMEM((half, 128), BF16),
            pltpu.VMEM((2, 2, part, 512), BF16),
            pltpu.VMEM((2, 2, 2, part, 512), BF16),
            pltpu.VMEM((2, 2, part, 512), BF16),
            pltpu.VMEM((2, 2, 2, part, 512), BF16),
            pltpu.VMEM((NY, 2, part, 512), BF16),
            pltpu.VMEM((2 * NY, part, 128), BF16),
            dma((8,)),
            dma((len(plan),)),
            dma((len(plan),)),
            dma((3,)),
            dma((3,)),
            dma((2,)),
            dma((2, 2)),
            dma((2, 2)),
            dma((2, 2, 2)),
            dma((2, 2, 2)),
            dma((2, 2, 2)),
            dma((2, 2, 2)),
            dma((7,)),
            dma((7,)),
        ],
        compiler_params=pltpu.CompilerParams(collective_id=0, has_side_effects=True),
        name="encoder",
    )(
        group_ids,
        tokens,
        w_qkv.reshape(width, 384),
        w_out,
        w_up,
        w_down,
        gain_one.reshape(1, -1),
        gain_two.reshape(1, -1),
        rel_table,
        prompt_cache.reshape(2, 2, PLEN, 128),
        w_proj,
    )


def slot_order(holders):
    count = holders.shape[0]
    same = holders[:, None] == holders[None, :]
    earlier = jnp.arange(count)[:, None] > jnp.arange(count)[None, :]
    return jnp.sum(same & earlier, axis=1)


def rate_slots(slot_query, slot_doc, doc_vectors, doc_lengths):
    shape = slot_doc.shape
    flat_doc = slot_doc.reshape(-1)
    flat_query = slot_query.reshape((flat_doc.shape[0],) + slot_query.shape[-2:])
    safe_doc = jnp.maximum(flat_doc, 0)
    documents = doc_vectors[safe_doc]
    lengths = doc_lengths[safe_doc]
    sims = jnp.einsum("sqe,sje->sqj", flat_query, documents, preferred_element_type=jnp.float32)
    live = jnp.arange(documents.shape[1], dtype=jnp.int32)[None, None, :] < lengths[:, None, None]
    best = jnp.max(jnp.where(live, sims, -jnp.inf), axis=2)
    totals = jnp.where(flat_doc >= 0, jnp.sum(best, axis=1), 0.0)
    return totals.reshape(shape)


def body(
    tokens,
    w_qkv,
    w_out,
    w_up,
    w_down,
    gain_one,
    gain_two,
    rel_table,
    prompt_cache,
    w_proj,
    doc_vectors,
    doc_lengths,
    group_ids,
    candidates,
):
    req_dev = tokens.shape[0] // QLEN
    query_vectors = encode(
        tokens, w_qkv, w_out, w_up, w_down, gain_one, gain_two, rel_table, prompt_cache, w_proj, group_ids
    )
    shards = lax.axis_size("doc")
    cand_dev = candidates.shape[1]
    pairs = req_dev * cand_dev
    capacity = max(2, 2 * pairs // shards)
    flat_cand = candidates.reshape(-1)
    holders = flat_cand // DOC_DEV
    request_of = jnp.arange(pairs, dtype=jnp.int32) // cand_dev
    slot_rank = slot_order(holders)
    copies, cand_copies = (
        lax.all_gather(query_vectors, "doc", axis=0, tiled=True),
        lax.all_gather(candidates, "doc", axis=0, tiled=True),
    )
    all_query = copies.reshape(shards, req_dev, QLEN, copies.shape[1])
    all_cand = cand_copies.reshape(shards, pairs)
    holder_all = all_cand // DOC_DEV
    local_all = all_cand % DOC_DEV
    rank_all = jax.vmap(slot_order)(holder_all)
    own_index = lax.axis_index("doc")
    chosen = (holder_all[:, None, :] == own_index) & (
        rank_all[:, None, :] == jnp.arange(capacity, dtype=jnp.int32)[None, :, None]
    )
    filled = jnp.any(chosen, axis=2)
    slot_request = jnp.sum(jnp.where(chosen, request_of[None, None, :], 0), axis=2)
    slot_doc = jnp.where(
        filled, jnp.sum(jnp.where(chosen, local_all[:, None, :], 0), axis=2), -1
    ).astype(jnp.int32)
    slot_query = all_query[jnp.arange(shards)[:, None], slot_request]
    slot_scores = rate_slots(slot_query, slot_doc, doc_vectors, doc_lengths)
    returned = lax.all_to_all(slot_scores, "doc", split_axis=0, concat_axis=0, tiled=True)
    scores = returned.reshape(-1)[holders * capacity + slot_rank].reshape(candidates.shape)
    return (query_vectors, scores)


def solution(mesh):
    placed = (
        P("doc", None),
        P(None, None, "head"),
        P("head", None),
        P(None, "head"),
        P("head", None),
        P(),
        P(),
        P(),
        P(None, "doc", "head"),
        P(),
        P("doc", None, None),
        P("doc"),
        P("doc"),
        P("doc", "head"),
    )
    return jax.shard_map(
        body,
        mesh=mesh,
        in_specs=placed,
        out_specs=(P("doc", None), P("doc", "head")),
        check_vma=False,
    )
```

time: 387 us -> 195 us (0.50)
  the two profiles are of different devices: /device:TPU:1 before, /device:TPU:8 now
where the time goes in v1:
time: 195 us
  Pallas kernels  67.9 us (35%)
  blocking collectives  41.6 us (21%)
  waiting for transfers between devices  30.4 us (16%)
  local copies, waits for them, and re-layouts  23.3 us (12%)
  between operations  14.2 us (7%)
  matrix products  9.2 us (5%)
  starting transfers between devices  5.27 us (3%)
  other arithmetic  2.83 us (1%)
    pallas_call x1, Pallas kernels, encode(): pl.pallas_call(functools.partial(encoder_kernel, plan), out_shape=jax.Sha...  67.9 us
    all_gather x1, blocking collectives, body(): lax.all_gather(candidates, 'doc', axis=0, tiled=True)  41.6 us
    all_gather x1, waiting for transfers between devices, body(): lax.all_gather(query_vectors, 'doc', axis=0, tiled=True)  20.7 us
    gather x1, local copies, waits for them, and re-layouts, rate_slots(): documents = doc_vectors[safe_doc]  10.5 us
    all_to_all x1, waiting for transfers between devices, body(): lax.all_to_all(slot_scores, 'doc', split_axis=0, concat_axis=0, tiled=True)  9.7 us
    dot_general x1, matrix products, rate_slots(): jnp.einsum('sqe,sje->sqj', flat_query, documents, preferred_element_type=...  9.2 us
    all_to_all x1, starting transfers between devices, body(): lax.all_to_all(slot_scores, 'doc', split_axis=0, concat_axis=0, tiled=True)  5.23 us
  transfers between devices with their start and end apart: 2, of which 2 were waited for; matrix products, arithmetic and copies ran while one was open for 8% of the time, Pallas kernels for 0%

profile of v1, /device:TPU:8, one launch (start us, length us, event | category | flops | bytes accessed | tf_op | source)
XLA Modules:
  0.0 194.8 jit_solution(4967955217671269705)
XLA Ops:
  7.2 1.4 copy.72
  8.6 1.2 copy.73.w_qkv_hbm
  9.8 67.9 %encoder.1 = bf16[384,128]{1,0:T(8,128)(2,1)} custom-call(s32[12]{0:T(128)} %group_ref.1, bf16[384,1024]{1,0:T(8,128)(2,1)} %tokens_hbm.1, bf16[1024,384]{1,0:T(8,128)(2,1)} %copy.73.w_qkv_hbm, bf16[128,1024]{1,0:T(8,128)(2,1)} %w_out_hbm.1, bf16[1024,512]{1,0:T(8,128)(2,1)} %w_up_hbm.1, bf16[512,1024]{1,0:T(8,128)(2,1)} %w_down_hbm.1, f32[1,1024]{1,0:T(1,128)} %bitcast.26, ...), custom_call_target="tpu_custom_call" | custom-call | tf_op jit(solution)/shard_map/encoder/pallas_call | solution.py:481
  78.0 41.6 %all-gather = s32[32,12,8]{1,2,0:T(8,128)S(1)} all-gather(s32[1,12,8]{1,2,0:T(8,128)S(1)} %bitcast.25), channel_id=1, replica_groups=mesh['head'=8,'doc'=32] {'doc'}, dimensions={0}, use_global_device_ids=true | all-gather | bytes 12672 | tf_op jit(solution)/shard_map/all_gather | solution.py:590
  119.6 0.1 copy.74
  119.9 1.2 convert_reduce_fusion
  121.0 0.2 fusion.1
  121.2 0.3 select_reduce_fusion.1
  122.0 1.6 gather_fusion
  123.5 10.5 %gather_fusion.2 = bf16[192,256,128]{2,1,0:T(8,128)(2,1)} fusion(bf16[64,256,128]{2,1,0:T(8,128)(2,1)} %param.24, s32[1024]{0:T(1024)S(1)} %pad_clamp_fusion.1), kind=kCustom, calls=%fused_computation.2 | custom fusion | bytes 25166592 | tf_op jit(solution)/shard_map/gather | solution.py:551
  134.0 0.2 convert_reduce_fusion.1
  134.3 20.7 %all-gather.3.cloned.1.call-done = bf16[12288,128]{1,0:T(8,128)(2,1)} async-done(((bf16[384,128]{1,0:T(8,128)(2,1)}), bf16[12288,128]{1,0:T(8,128)(2,1)}) %all-gather.3.cloned.1.call-update) | async-done | bytes 3145744 | tf_op jit(solution)/shard_map/all_gather | solution.py:589
  155.1 3.7 %gather_fusion.1 = bf16[192,32,128]{2,1,0:T(8,128)(2,1)S(1)} fusion(bf16[32,12,32,128]{3,2,1,0:T(8,128)(2,1)} %bitcast.22, s32[192]{0:T(256)S(1)} %reshape.391), kind=kCustom, calls=%fused_computation.1 | custom fusion | bytes 3147264 | tf_op jit(solution)/shard_map/gather | solution.py:606
  158.8 9.2 %select_reduce_fusion = f32[192,32]{1,0:T(8,128)S(1)} fusion(pred[192,256]{1,0:T(8,128)(4,1)S(1)} %iota_compare_fusion, bf16[192,32,128]{2,1,0:T(8,128)(2,1)S(1)} %gather_fusion.1, bf16[192,256,128]{2,1,0:T(8,128)(2,1)} %gather_fusion.2), kind=kOutput, calls=%fused_computation.4 | convolution fusion | flops 405792768 | bytes 14229504 | tf_op jit(solution)/shard_map/sqe,sje->sqj/dot_general | solution.py:553
  168.0 0.1 reduce_sum.55
  168.1 0.1 reduce_sum.56
  168.3 0.7 copy.83
  169.0 5.2 %all-to-all-start = ((f32[32,1,6]{2,1,0:T(1,128)}), f32[32,1,6]{2,1,0:T(1,128)S(1)}, u32[]{:S(2)}, u32[]{:S(2)}) async-start(f32[32,1,6]{2,1,0:T(1,128)} %copy.83), calls=%async_computation | async-start | bytes 32768 | tf_op jit(solution)/shard_map/all_to_all | solution.py:608
  174.2 9.7 %all-to-all-done = f32[32,1,6]{2,1,0:T(1,128)S(1)} async-done(((f32[32,1,6]{2,1,0:T(1,128)}), f32[32,1,6]{2,1,0:T(1,128)S(1)}, u32[]{:S(2)}, u32[]{:S(2)}) %all-to-all-start) | async-done | bytes 800 | tf_op jit(solution)/shard_map/all_to_all | solution.py:608
  183.9 0.5 broadcast.373
  184.4 0.7 reduce.3
  185.2 1.3 gather_fusion.3
  186.6 0.7 copy.86
  187.3 0.6 copy.89
  (31 shorter events, 1.3 us)
Async XLA Ops:
  7.2 114.8 %copy-start = (s32[64]{0:T(128)S(1)}, s32[64]{0:T(128)}, u32[]{:S(2)}) copy-start(s32[64]{0:T(128)} %param.25) | copy-start | bytes 772
  7.2 147.9 %all-gather.3.cloned.1.call-start = ((), (), s32[]{:S(2)}) async-start(), calls=%async_computation.1 | async-start | bytes 3244032 | tf_op jit(solution)/shard_map/all_gather | solution.py:589
  9.8 67.9 %copy-start.2 = (s32[12,8]{0,1:T(8,128)S(1)}, s32[12,8]{0,1:T(8,128)}, u32[]{:S(2)}) copy-start(s32[12,8]{0,1:T(8,128)} %param.27) | copy-start | bytes 1156
  158.8 28.5 %copy-start.1 = (bf16[384,128]{1,0:T(8,128)(2,1)S(1)}, bf16[384,128]{1,0:T(8,128)(2,1)}, u32[]{:S(2)}) copy-start(bf16[384,128]{1,0:T(8,128)(2,1)} %encoder.1) | copy-start | bytes 294916
  169.0 14.9 %all-to-all-start = ((f32[32,1,6]{2,1,0:T(1,128)}), f32[32,1,6]{2,1,0:T(1,128)S(1)}, u32[]{:S(2)}, u32[]{:S(2)}) async-start(f32[32,1,6]{2,1,0:T(1,128)} %copy.83), calls=%async_computation | async-start | bytes 32768 | tf_op jit(solution)/shard_map/all_to_all | solution.py:608
Sparse Core Ops, SparseCore 0:
  77.8 77.2 all-gather.2

commit v2 on v1

--- a/solution.py
+++ b/solution.py
@@ -16,6 +16,7 @@
 NX = 4
 NZ = 8
 NY = 4
+SLOTS = 6
 MESH = pl.DeviceIdType.MESH
 F32 = jnp.float32
 BF16 = jnp.bfloat16
@@ -114,7 +115,11 @@
     rel_hbm,
     cache_hbm,
     w_proj_ref,
+    docs_hbm,
+    lengths_ref,
+    cand_hbm,
     query_out,
+    score_out,
     cache,
     tokens,
     w_qkv,
@@ -149,6 +154,25 @@
     hid_recv_sem,
     vec_send_sem,
     vec_recv_sem,
+    docs,
+    queries,
+    cand_rows,
+    table,
+    table_smem,
+    best_rows,
+    back_send,
+    back_recv,
+    table_sem,
+    cand_send_sem,
+    cand_recv_sem,
+    spread_send_sem,
+    spread_recv_sem,
+    across_send_sem,
+    across_recv_sem,
+    share_send_sem,
+    share_recv_sem,
+    back_send_sem,
+    back_recv_sem,
 ):
     head = lax.axis_index("head")
     doc = lax.axis_index("doc")
@@ -185,6 +209,7 @@
         pltpu.make_async_copy(w_out_hbm, w_out.at[core], load_sem.at[5]),
         pltpu.make_async_copy(w_up_hbm, w_up.at[core], load_sem.at[6]),
         pltpu.make_async_copy(w_down_hbm, w_down.at[core], load_sem.at[7]),
+        pltpu.make_async_copy(docs_hbm, docs, load_sem.at[8]),
     ]
     for load in loads:
         load.start()
@@ -415,6 +440,24 @@
     send_hidden(1, 0, 1)
     send_hidden(0, 0, 1)
     send_hidden(1, 0, 0)
+    home = mod(x + z, NY)
+    at_home = home == y
+    my_row = (x * 2 + lax.div(z, 4)) * NY + y
+
+    def cand_copy(offset):
+        return pltpu.make_async_remote_copy(
+            src_ref=cand_hbm,
+            dst_ref=cand_rows.at[my_row],
+            send_sem=cand_send_sem.at[offset],
+            recv_sem=cand_recv_sem.at[my_row],
+            device_id=(2 * home + core, mod(doc + offset, NX * NZ)),
+            device_id_type=MESH,
+        )
+
+    cand_local = pltpu.make_async_copy(cand_hbm, cand_rows.at[my_row], cand_recv_sem.at[my_row])
+    pl.when(at_home)(lambda: cand_local.start())
+    pl.when(jnp.logical_not(at_home))(lambda: cand_copy(0).start())
+    pl.loop(1, NX * NZ)(lambda offset: cand_copy(offset).start())
     for i in (6, 7):
         loads[i].wait()
     swaps[1].wait_recv()
@@ -437,6 +480,33 @@
     hidden_copy(0, 0, 1).wait_recv()
     hidden_copy(1, 0, 0).wait_recv()
     feed_up, feed_down = feed(y_up), feed(y_down)
+    @pl.loop(0, NX * NZ)
+    def _(row):
+        pltpu.make_async_copy(cand_hbm, cand_rows.at[row], cand_recv_sem.at[row]).wait()
+
+    lane = lax.broadcasted_iota(jnp.int32, (NX * NZ, 128), 1)
+    named = cand_rows[...].reshape(NX * NZ, 128)
+    mine = jnp.logical_and(lax.shift_right_logical(named, 6) == doc, lane < 96)
+    mine_f = jnp.where(mine, 1.0, 0.0)
+    before = (
+        lax.broadcasted_iota(jnp.int32, (128, 128), 0) < lax.broadcasted_iota(jnp.int32, (128, 128), 1)
+    ).astype(F32).astype(BF16)
+    rank = jnp.dot(mine_f.astype(BF16), before, preferred_element_type=F32)
+    rows_table = jnp.zeros((NX * NZ, 128), jnp.int32)
+    places = []
+    for slot in range(SLOTS):
+        chosen = jnp.where(rank == float(slot), mine_f, 0.0)
+        some = jnp.sum(chosen, axis=1, keepdims=True)
+        place = jnp.sum(chosen * lane.astype(F32), axis=1, keepdims=True).astype(jnp.int32)
+        which = jnp.sum(
+            chosen * lax.bitwise_and(named, DOC_DEV - 1).astype(F32), axis=1, keepdims=True
+        ).astype(jnp.int32)
+        places.append(jnp.where(some > 0.5, place, 127))
+        rows_table = jnp.where(lane == slot, lax.shift_right_logical(place, 3) * 2, rows_table)
+        rows_table = jnp.where(lane == slot + 8, which, rows_table)
+    table[...] = rows_table
+    table_copy = pltpu.make_async_copy(table, table_smem, table_sem.at[0])
+    table_copy.start()
     hidden_copy(0, 1, 0).wait_recv()
     hidden_copy(1, 1, 1).wait_recv()
     total_two, sent_three = reduce_rows(
@@ -445,7 +515,7 @@
     two = norm_rows(one.astype(F32) + total_two, gain_two_ref[...]).astype(BF16)
     projected = jnp.dot(two, w_proj_ref[...], preferred_element_type=F32)
     unit = projected * lax.rsqrt(jnp.sum(projected * projected, axis=-1, keepdims=True) + 1e-06)
-    vectors[head] = unit.astype(BF16)
+    vectors[head] = unit.astype(BF16).reshape(3, 16, 128)
 
     sent_four = []
     for i, device in enumerate(peers):
@@ -459,17 +529,166 @@
         )
         copy.start()
         sent_four.append(copy)
+    half_doc = lax.div(z, 4)
+    piece_rows = pl.ds(core * 12 + y * 3, 3)
+
+    def spread_copy(offset):
+        return pltpu.make_async_remote_copy(
+            src_ref=vectors.at[head],
+            dst_ref=queries.at[x * 2 + half_doc, piece_rows],
+            send_sem=spread_send_sem.at[offset],
+            recv_sem=spread_recv_sem.at[half_doc, y],
+            device_id=(2 * home + core, x * NZ + mod(z + offset, NZ)),
+            device_id_type=MESH,
+        )
+
+    def across_copy(half_index, source_y, offset, index):
+        rows = queries.at[index, pl.ds(core * 12 + source_y * 3, 3)]
+        return pltpu.make_async_remote_copy(
+            src_ref=rows,
+            dst_ref=rows,
+            send_sem=across_send_sem.at[half_index, source_y, offset - 1],
+            recv_sem=across_recv_sem.at[half_index, source_y, offset - 1],
+            device_id=(head, mod(x + offset, NX) * NZ + z),
+            device_id_type=MESH,
+        )
+
+    def share_copy(place, index):
+        rows = queries.at[index, pl.ds(core * 12, 12)]
+        return pltpu.make_async_remote_copy(
+            src_ref=rows,
+            dst_ref=rows,
+            send_sem=share_send_sem.at[place],
+            recv_sem=share_recv_sem.at[place],
+            device_id=partner,
+            device_id_type=MESH,
+        )
+
+    spread_local = pltpu.make_async_copy(
+        vectors.at[head], queries.at[x * 2 + half_doc, piece_rows], spread_recv_sem.at[half_doc, y]
+    )
+    pl.when(at_home)(lambda: spread_local.start())
+    pl.when(jnp.logical_not(at_home))(lambda: spread_copy(0).start())
+    for offset in (4, 3, 5, 2, 6, 1, 7):
+        spread_copy(offset).start()
+    crossing = []
+    shared = []
+    for source_y in range(NY):
+        for half_index in range(2):
+            pltpu.make_async_copy(
+                vectors.at[head],
+                queries.at[x * 2 + half_index, pl.ds(core * 12 + source_y * 3, 3)],
+                spread_recv_sem.at[half_index, source_y],
+            ).wait()
+            for offset in (2, 1, 3):
+                crossing.append(across_copy(half_index, source_y, offset, x * 2 + half_index))
+                crossing[-1].start()
+    for half_index in range(2):
+        shared.append(share_copy(half_index, x * 2 + half_index))
+        shared[-1].start()
     for copy in sent_four:
         copy.wait_recv()
     for block in range(2 * NY):
         place = (block % 2) * half + (block // 2) * part
-        query_out[place : place + part, :] = vectors[block]
-
-    for copy in list(copies.values()) + swaps + [att_copy] + sent_one + sent_two + sent_three + sent_four:
+        query_out[place : place + part, :] = vectors[block].reshape(part, 128)
+    for offset in (1, 3, 2):
+        for half_index in range(2):
+            index = mod(x - offset, NX) * 2 + half_index
+            for source_y in range(NY):
+                across_copy(half_index, source_y, offset, index).wait_recv()
+            shared.append(share_copy(2 * offset + half_index, index))
+            shared[-1].start()
+    table_copy.wait()
+    loads[8].wait()
+    for copy in shared:
+        copy.wait_recv()
+
+    zeros = jnp.zeros((QLEN, 128), BF16)
+    row_index = lax.broadcasted_iota(jnp.int32, (256, 2 * QLEN), 0)
+    first_lanes = lax.broadcasted_iota(jnp.int32, (1, 2 * QLEN), 1) < QLEN
+
+    @pl.loop(0, NX * NZ)
+    def _(row):
+        source = lax.div(row, NY)
+        for pair in range(SLOTS // 2):
+            found = []
+            for slot in (2 * pair, 2 * pair + 1):
+                which = jnp.clip(table_smem[row, slot + 8], 0, DOC_DEV - 1)
+                request = jnp.clip(table_smem[row, slot], 0, 22)
+                query = jnp.concatenate([queries[source, request], queries[source, request + 1]], axis=0)
+                found.append((docs[which], query, lengths_ref[which]))
+            (doc_a, query_a, len_a), (doc_b, query_b, len_b) = found
+            left = jnp.concatenate([doc_a, doc_b], axis=1)
+            right = jnp.concatenate(
+                [
+                    jnp.concatenate([query_a, zeros], axis=1),
+                    jnp.concatenate([zeros, query_b], axis=1),
+                ],
+                axis=0,
+            )
+            sims = lax.dot_general(left, right, NT, preferred_element_type=F32)
+            live = row_index < jnp.where(first_lanes, len_a, len_b)
+            best_rows[pair, pl.ds(row, 1), : 2 * QLEN] = jnp.max(
+                jnp.where(live, sims, -jnp.inf), axis=0, keepdims=True
+            )
+
+    rated = jnp.zeros((NX * NZ, 128), F32)
+    for slot in range(SLOTS):
+        low = (slot % 2) * QLEN
+        value = jnp.sum(best_rows[slot // 2][:, low : low + QLEN], axis=1, keepdims=True)
+        rated = rated + jnp.where(lane == places[slot], value, 0.0)
+    back_send[...] = rated.reshape(NX * NZ, 1, 128)
+
+    def back_to(row):
+        source_x, source_half, source_y = lax.div(row, 8), lax.rem(lax.div(row, NY), 2), lax.rem(row, NY)
+        source = source_x * NZ + mod(y - source_x, NY) + 4 * source_half
+        return source, source_y
+
+    def back_copy(row):
+        source, source_y = back_to(row)
+        return pltpu.make_async_remote_copy(
+            src_ref=back_send.at[row],
+            dst_ref=back_recv.at[doc],
+            send_sem=back_send_sem.at[row],
+            recv_sem=back_recv_sem.at[doc],
+            device_id=(2 * source_y + core, source),
+            device_id_type=MESH,
+        )
+
+    def is_own(row):
+        source, source_y = back_to(row)
+        return jnp.logical_and(source == doc, source_y == y)
+
+    @pl.loop(0, NX * NZ)
+    def _(row):
+        own_row = is_own(row)
+        pl.when(own_row)(
+            lambda: pltpu.make_async_copy(
+                back_send.at[row], back_recv.at[doc], back_recv_sem.at[doc]
+            ).start()
+        )
+        pl.when(jnp.logical_not(own_row))(lambda: back_copy(row).start())
+
+    @pl.loop(0, NX * NZ)
+    def _(row):
+        pltpu.make_async_copy(back_send.at[0], back_recv.at[row], back_recv_sem.at[row]).wait()
+
+    score_out[...] = jnp.sum(back_recv[...], axis=0)
+
+    @pl.loop(0, NX * NZ)
+    def _(row):
+        pl.when(jnp.logical_not(is_own(row)))(lambda: back_copy(row).wait_send())
+
+    pl.when(jnp.logical_not(at_home))(lambda: cand_copy(0).wait_send())
+    pl.loop(1, NX * NZ)(lambda offset: cand_copy(offset).wait_send())
+    pl.when(jnp.logical_not(at_home))(lambda: spread_copy(0).wait_send())
+    for offset in range(1, NZ):
+        spread_copy(offset).wait_send()
+    for copy in list(copies.values()) + swaps + [att_copy] + sent_one + sent_two + sent_three + sent_four + crossing + shared:
         copy.wait_send()
 
 
-def encode(tokens, w_qkv, w_out, w_up, w_down, gain_one, gain_two, rel_table, prompt_cache, w_proj, group_ids):
+def encode(tokens, w_qkv, w_out, w_up, w_down, gain_one, gain_two, rel_table, prompt_cache, w_proj, docs, lengths, named, group_ids):
     plan = plan_gather()
     rows, width = tokens.shape
     half = rows // 2
@@ -480,9 +699,9 @@
     dma = pltpu.SemaphoreType.DMA
     return pl.pallas_call(
         functools.partial(encoder_kernel, plan),
-        out_shape=jax.ShapeDtypeStruct((rows, 128), BF16),
-        in_specs=[smem] + [anywhere] * 5 + [vmem, vmem, anywhere, anywhere, vmem],
-        out_specs=vmem,
+        out_shape=(jax.ShapeDtypeStruct((rows, 128), BF16), jax.ShapeDtypeStruct((1, 128), F32)),
+        in_specs=[smem] + [anywhere] * 5 + [vmem, vmem, anywhere, anywhere, vmem, anywhere, smem, anywhere],
+        out_specs=(vmem, vmem),
         scratch_shapes=[
             pltpu.VMEM((2, 64, PLEN, 128), BF16),
             pltpu.VMEM((rows, width), BF16),
@@ -503,8 +722,8 @@
             pltpu.VMEM((2, 2, part, 512), BF16),
             pltpu.VMEM((2, 2, 2, part, 512), BF16),
             pltpu.VMEM((NY, 2, part, 512), BF16),
-            pltpu.VMEM((2 * NY, part, 128), BF16),
-            dma((8,)),
+            pltpu.VMEM((2 * NY, 3, 16, 128), BF16),
+            dma((9,)),
             dma((len(plan),)),
             dma((len(plan),)),
             dma((3,)),
@@ -518,6 +737,25 @@
             dma((2, 2, 2)),
             dma((7,)),
             dma((7,)),
+            pltpu.VMEM((64, 256, 128), BF16),
+            pltpu.VMEM((8, 24, 16, 128), BF16),
+            pltpu.VMEM((32, 1, 128), jnp.int32),
+            pltpu.VMEM((32, 128), jnp.int32),
+            pltpu.SMEM((32, 128), jnp.int32),
+            pltpu.VMEM((SLOTS // 2, 32, 128), F32),
+            pltpu.VMEM((32, 1, 128), F32),
+            pltpu.VMEM((32, 1, 128), F32),
+            dma((1,)),
+            dma((32,)),
+            dma((32,)),
+            dma((8,)),
+            dma((2, 4)),
+            dma((2, 4, 3)),
+            dma((2, 4, 3)),
+            dma((8,)),
+            dma((8,)),
+            dma((32,)),
+            dma((32,)),
         ],
         compiler_params=pltpu.CompilerParams(collective_id=0, has_side_effects=True),
         name="encoder",
@@ -533,28 +771,10 @@
         rel_table,
         prompt_cache.reshape(2, 2, PLEN, 128),
         w_proj,
+        docs,
+        lengths,
+        named,
     )
-
-
-def slot_order(holders):
-    count = holders.shape[0]
-    same = holders[:, None] == holders[None, :]
-    earlier = jnp.arange(count)[:, None] > jnp.arange(count)[None, :]
-    return jnp.sum(same & earlier, axis=1)
-
-
-def rate_slots(slot_query, slot_doc, doc_vectors, doc_lengths):
-    shape = slot_doc.shape
-    flat_doc = slot_doc.reshape(-1)
-    flat_query = slot_query.reshape((flat_doc.shape[0],) + slot_query.shape[-2:])
-    safe_doc = jnp.maximum(flat_doc, 0)
-    documents = doc_vectors[safe_doc]
-    lengths = doc_lengths[safe_doc]
-    sims = jnp.einsum("sqe,sje->sqj", flat_query, documents, preferred_element_type=jnp.float32)
-    live = jnp.arange(documents.shape[1], dtype=jnp.int32)[None, None, :] < lengths[:, None, None]
-    best = jnp.max(jnp.where(live, sims, -jnp.inf), axis=2)
-    totals = jnp.where(flat_doc >= 0, jnp.sum(best, axis=1), 0.0)
-    return totals.reshape(shape)
 
 
 def body(
@@ -573,41 +793,24 @@
     group_ids,
     candidates,
 ):
-    req_dev = tokens.shape[0] // QLEN
-    query_vectors = encode(
-        tokens, w_qkv, w_out, w_up, w_down, gain_one, gain_two, rel_table, prompt_cache, w_proj, group_ids
+    named = jnp.pad(candidates.reshape(1, -1), ((0, 0), (0, 128 - candidates.size)), constant_values=-1)
+    query_vectors, rated = encode(
+        tokens,
+        w_qkv,
+        w_out,
+        w_up,
+        w_down,
+        gain_one,
+        gain_two,
+        rel_table,
+        prompt_cache,
+        w_proj,
+        doc_vectors,
+        doc_lengths,
+        named,
+        group_ids,
     )
-    shards = lax.axis_size("doc")
-    cand_dev = candidates.shape[1]
-    pairs = req_dev * cand_dev
-    capacity = max(2, 2 * pairs // shards)
-    flat_cand = candidates.reshape(-1)
-    holders = flat_cand // DOC_DEV
-    request_of = jnp.arange(pairs, dtype=jnp.int32) // cand_dev
-    slot_rank = slot_order(holders)
-    copies, cand_copies = (
-        lax.all_gather(query_vectors, "doc", axis=0, tiled=True),
-        lax.all_gather(candidates, "doc", axis=0, tiled=True),
-    )
-    all_query = copies.reshape(shards, req_dev, QLEN, copies.shape[1])
-    all_cand = cand_copies.reshape(shards, pairs)
-    holder_all = all_cand // DOC_DEV
-    local_all = all_cand % DOC_DEV
-    rank_all = jax.vmap(slot_order)(holder_all)
-    own_index = lax.axis_index("doc")
-    chosen = (holder_all[:, None, :] == own_index) & (
-        rank_all[:, None, :] == jnp.arange(capacity, dtype=jnp.int32)[None, :, None]
-    )
-    filled = jnp.any(chosen, axis=2)
-    slot_request = jnp.sum(jnp.where(chosen, request_of[None, None, :], 0), axis=2)
-    slot_doc = jnp.where(
-        filled, jnp.sum(jnp.where(chosen, local_all[:, None, :], 0), axis=2), -1
-    ).astype(jnp.int32)
-    slot_query = all_query[jnp.arange(shards)[:, None], slot_request]
-    slot_scores = rate_slots(slot_query, slot_doc, doc_vectors, doc_lengths)
-    returned = lax.all_to_all(slot_scores, "doc", split_axis=0, concat_axis=0, tiled=True)
-    scores = returned.reshape(-1)[holders * capacity + slot_rank].reshape(candidates.shape)
-    return (query_vectors, scores)
+    return (query_vectors, rated[0, : candidates.size].reshape(candidates.shape))
 
 
 def solution(mesh):

time: 195 us -> 102 us (0.52)
  the two profiles are of different devices: /device:TPU:8 before, /device:TPU:1 now
where the time goes in v2:
time: 102 us; the launch traced here: 101 us
  Pallas kernels  93.6 us (92%)
  local copies, waits for them, and re-layouts  6.84 us (7%)
    pallas_call x1, Pallas kernels, encode(): pl.pallas_call(functools.partial(encoder_kernel, plan), out_shape=(jax.Sh...  93.6 us
    unnamed x4, local copies, waits for them, and re-layouts  4.39 us

profile of v2, /device:TPU:1, one launch (start us, length us, event | category | flops | bytes accessed | tf_op | source)
XLA Modules:
  0.0 101.1 jit_solution(62146215230484477)
XLA Ops:
  0.6 1.4 %copy.19 = bf16[1024,3,128]{0,2,1:T(8,128)(2,1)S(1)} copy(bf16[1024,3,128]{2,0,1:T(8,128)(2,1)} %param.15) | data formatting | bytes 1572864 | tf_op args[1]
  2.0 1.2 %copy.21.w_qkv_hbm = bf16[1024,384]{1,0:T(8,128)(2,1)} copy(bf16[1024,384]{0,1:T(8,128)(2,1)S(1)} %bitcast.4) | data formatting | bytes 1572864 | tf_op jit(solution)/shard_map/reshape | solution.py:765
  3.2 0.8 copy.20
  4.0 0.1 reshape.23
  4.0 0.5 pad.4.cand_hbm
  4.6 93.6 %encoder.1 = (bf16[384,128]{1,0:T(8,128)(2,1)}, f32[1,128]{1,0:T(1,128)}) custom-call(s32[12]{0:T(128)} %group_ref.1, bf16[384,1024]{1,0:T(8,128)(2,1)} %tokens_hbm.1, bf16[1024,384]{1,0:T(8,128)(2,1)} %copy.21.w_qkv_hbm, bf16[128,1024]{1,0:T(8,128)(2,1)} %w_out_hbm.1, bf16[1024,512]{1,0:T(8,128)(2,1)} %w_up_hbm.1, bf16[512,1024]{1,0:T(8,128)(2,1)} %w_down_hbm.1, ...), custom_call_target="tpu_custom_call" | custom-call | tf_op jit(solution)/shard_map/encoder/pallas_call | solution.py:700
  98.2 0.6 slice_reduce_fusion
  98.8 0.1 reshape_squeeze.3
  98.9 0.7 copy.22
  99.5 1.5 %copy.24 = bf16[384,128]{1,0:T(8,128)(2,1)} copy(bf16[384,128]{1,0:T(8,128)(2,1)} %get-tuple-element.12) | data formatting | bytes 196608

commit v3 on v2

--- a/solution.py
+++ b/solution.py
@@ -17,6 +17,7 @@
 NZ = 8
 NY = 4
 SLOTS = 6
+ROWS = 4
 MESH = pl.DeviceIdType.MESH
 F32 = jnp.float32
 BF16 = jnp.bfloat16
@@ -27,10 +28,17 @@
     return lax.rem(value + 4 * size, size)
 
 
+HOP_US = 2.3
+ROUTE_US = 0.65
+ROWS_US = 256 / 46500.0
+Z_FIRST = ((0, 0, 128),)
+X_FIRST = ((1, 0, 128),)
+
+
 class Message:
-    def __init__(self, kv, axis, sign, dx, dz, low, rows, parent):
-        self.kv, self.axis, self.sign, self.dx, self.dz = kv, axis, sign, dx, dz
-        self.low, self.rows, self.parent = low, rows, parent
+    def __init__(self, kv, axis, sign, hops, dx, dz, low, rows, parent):
+        self.kv, self.axis, self.sign, self.hops = kv, axis, sign, hops
+        self.dx, self.dz, self.low, self.rows, self.parent = dx, dz, low, rows, parent
         self.children = []
         self.time = None
         self.index = None
@@ -39,39 +47,41 @@
 def plan_gather():
     made = []
 
-    def add(kv, axis, sign, dx, dz, low, rows, parent):
-        message = Message(kv, axis, sign, dx, dz, low, rows, parent)
-        made.append(message)
-        return message
-
-    def along_x(kv, dz, low, rows, parent):
+    def add(*fields):
+        made.append(Message(*fields))
+        return made[-1]
+
+    def along_x(kv, dz, low, rows, parent, direct):
         out = []
+        half = rows // 2
         for sign in (1, -1):
-            near = add(kv, "x", sign, sign, dz, low, rows, parent)
-            half = rows // 2
-            far = add(kv, "x", sign, 2 * sign, dz, low if sign > 0 else low + half, half, near)
-            out += [near, far]
+            near = add(kv, "x", sign, 1, sign, dz, low, rows, parent)
+            part = low if sign > 0 else low + half
+            hops = 2 if direct else 1
+            out += [near, add(kv, "x", sign, hops, 2 * sign, dz, part, half, parent if direct else near)]
         return out
 
-    def along_z(kv, dx, low, rows, parent):
+    def along_z(kv, dx, low, rows, parent, jump):
         out = []
+        half = rows // 2
         for sign in (1, -1):
-            previous = parent
-            for step in range(1, 4):
-                previous = add(kv, "z", sign, dx, sign * step, low, rows, previous)
-                out.append(previous)
-            half = rows // 2
-            out.append(add(kv, "z", sign, dx, sign * 4, low if sign > 0 else low + half, half, previous))
+            one = add(kv, "z", sign, 1, dx, sign, low, rows, parent)
+            two = add(kv, "z", sign, 2 if jump else 1, dx, 2 * sign, low, rows, parent if jump else one)
+            three = add(kv, "z", sign, 1, dx, 3 * sign, low, rows, two)
+            part = low if sign > 0 else low + half
+            out += [one, two, three, add(kv, "z", sign, 1, dx, 4 * sign, part, half, three)]
         return out
 
-    firsts = along_z(0, 0, 0, 128, None)
-    along_x(0, 0, 0, 128, None)
-    for first in firsts:
-        along_x(0, first.dz, first.low, first.rows, first)
-    firsts = along_x(1, 0, 0, 128, None)
-    along_z(1, 0, 0, 128, None)
-    for first in firsts:
-        along_z(1, first.dx, first.low, first.rows, first)
+    for kv, low, rows in Z_FIRST:
+        firsts = along_z(kv, 0, low, rows, None, True)
+        along_x(kv, 0, low, rows, None, False)
+        for first in firsts:
+            along_x(kv, first.dz, first.low, first.rows, first, False)
+    for kv, low, rows in X_FIRST:
+        firsts = along_x(kv, 0, low, rows, None, True)
+        along_z(kv, 0, low, rows, None, False)
+        for first in firsts:
+            along_z(kv, first.dx, first.low, first.rows, first, False)
     for message in made:
         if message.parent is not None:
             message.parent.children.append(message)
@@ -82,9 +92,8 @@
         start, i = ready.pop(0)
         message = made[i]
         link = (message.axis, message.sign)
-        begin = max(start, free.get(link, 0.0))
-        free[link] = begin + message.rows * 256 / 46500.0
-        message.time = free[link] + 1.6
+        free[link] = max(start, free.get(link, 0.0)) + message.rows * ROWS_US * message.hops
+        message.time = free[link] + HOP_US + ROUTE_US * (message.hops - 1)
         ready += [(message.time, made.index(child)) for child in message.children]
     order = sorted(made, key=lambda m: m.time)
     for index, message in enumerate(order):
@@ -104,22 +113,30 @@
 
 def encoder_kernel(
     plan,
-    group_ref,
+    group_hbm,
     tokens_hbm,
     w_qkv_hbm,
     w_out_hbm,
     w_up_hbm,
     w_down_hbm,
-    gain_one_ref,
-    gain_two_ref,
+    gain_one_hbm,
+    gain_two_hbm,
     rel_hbm,
     cache_hbm,
-    w_proj_ref,
+    w_proj_hbm,
     docs_hbm,
-    lengths_ref,
+    lengths_hbm,
     cand_hbm,
     query_out,
     score_out,
+    group_ref,
+    gains,
+    w_proj,
+    lengths_ref,
+    cand_tile,
+    cand_wide,
+    cand_mine,
+    score_tile,
     cache,
     tokens,
     w_qkv,
@@ -193,7 +210,7 @@
     peers = [partner]
     for other in (y_up, y_down, y_far):
         peers += [(2 * other + core, doc), (2 * other + 1 - core, doc)]
-    links = [at_link(axis, sign) for axis in ("x", "z") for sign in (1, -1)]
+    links = [at_link(axis, sign * hops) for axis in ("x", "z") for sign in (1, -1) for hops in (1, 2)]
     barrier = pltpu.get_barrier_semaphore()
     for device in peers + links:
         pl.semaphore_signal(barrier, inc=1, device_id=device, device_id_type=MESH)
@@ -210,6 +227,12 @@
         pltpu.make_async_copy(w_up_hbm, w_up.at[core], load_sem.at[6]),
         pltpu.make_async_copy(w_down_hbm, w_down.at[core], load_sem.at[7]),
         pltpu.make_async_copy(docs_hbm, docs, load_sem.at[8]),
+        pltpu.make_async_copy(gain_one_hbm, gains.at[pl.ds(0, 1)], load_sem.at[9]),
+        pltpu.make_async_copy(gain_two_hbm, gains.at[pl.ds(8, 1)], load_sem.at[10]),
+        pltpu.make_async_copy(w_proj_hbm, w_proj, load_sem.at[11]),
+        pltpu.make_async_copy(lengths_hbm, lengths_ref, load_sem.at[12]),
+        pltpu.make_async_copy(cand_hbm, cand_tile, load_sem.at[13]),
+        pltpu.make_async_copy(group_hbm, group_ref, load_sem.at[14]),
     ]
     for load in loads:
         load.start()
@@ -218,22 +241,26 @@
     def gather_copy(message):
         dx, dz = message.dx, message.dz
         if message.axis == "x":
-            dx -= message.sign
+            dx -= message.sign * message.hops
         else:
-            dz -= message.sign
+            dz -= message.sign * message.hops
         block = mod(x - dx, NX) * NZ + mod(z - dz, NZ)
         group, low = block * 2 + message.low // PLEN, message.low % PLEN
         if message.rows == 2 * PLEN:
             target = cache.at[message.kv, pl.ds(group, 2)]
         else:
             target = cache.at[message.kv, group, pl.ds(low, message.rows)]
-        source = cache_hbm.at[message.kv] if message.parent is None else target
+        source = target
+        if message.parent is None:
+            source = cache_hbm.at[message.kv]
+            if message.rows < 2 * PLEN:
+                source = source.at[message.low // PLEN, pl.ds(low, message.rows)]
         return pltpu.make_async_remote_copy(
             src_ref=source,
             dst_ref=target,
             send_sem=gather_send.at[message.index],
             recv_sem=gather_recv.at[message.index],
-            device_id=at_link(message.axis, message.sign),
+            device_id=at_link(message.axis, message.sign * message.hops),
             device_id_type=MESH,
         )
 
@@ -261,12 +288,13 @@
     low_head = lax.broadcasted_iota(jnp.int32, (128, 128), 1) < HD
     for block in range(3):
         rows = slice(block * 128, block * 128 + 128)
-        made = jnp.dot(tokens[rows, :], w_qkv[...], preferred_element_type=F32)
-        q_made = made[:, :128]
+        q_made, k_made, v_made = (
+            jnp.dot(tokens[rows, :], w_qkv[i], preferred_element_type=F32) for i in range(3)
+        )
         q_mask[0, rows, :] = jnp.where(low_head, q_made, 0.0).astype(BF16)
         q_mask[1, rows, :] = jnp.where(low_head, 0.0, q_made).astype(BF16)
-        k_own[rows, :] = made[:, 128:256].astype(BF16)
-        v_own[rows, :] = made[:, 256:].astype(BF16)
+        k_own[rows, :] = k_made.astype(BF16)
+        v_own[rows, :] = v_made.astype(BF16)
     loads[2].wait()
     loads[3].wait()
     flip = (
@@ -275,7 +303,7 @@
     ).astype(F32).astype(BF16)
     for i in range(2):
         row = jnp.dot(
-            rel[i], w_qkv[:, i * 128 : i * 128 + 128], preferred_element_type=F32
+            rel[i], w_qkv[i], preferred_element_type=F32
         ).astype(BF16)
         turned = jnp.dot(flip, row, preferred_element_type=F32)
         rel_two[i, 0:128, :] = jnp.where(low_head, turned, 0.0).astype(BF16)
@@ -285,6 +313,11 @@
         q_all = q_mask[0, rows, :] + q_mask[1, rows, :]
         q_rel[rows, :] = lax.dot_general(q_all, rel_two[1], NT, preferred_element_type=F32)
     loads[4].wait()
+    for i in range(9, 15):
+        loads[i].wait()
+    cand_wide[...] = jnp.zeros_like(cand_wide)
+    cand_wide[:, : cand_tile.shape[1]] = cand_tile[...]
+    cand_mine[...] = jnp.sum(pltpu.roll(cand_wide[...], 0, 1, stride=16, stride_axis=0), axis=0, keepdims=True)
 
     for message in plan:
         copies[message.index].wait_recv()
@@ -414,7 +447,7 @@
         lambda: out_part(y),
     )
     own_rows = pl.ds(pl.multiple_of(core * half + y * part, 16), part)
-    one = norm_rows(tokens[own_rows, :].astype(F32) + total, gain_one_ref[...]).astype(BF16)
+    one = norm_rows(tokens[own_rows, :].astype(F32) + total, gains[0:1, :]).astype(BF16)
     for piece in range(2):
         hidden[y, piece] = one[:, piece * wide : piece * wide + wide]
 
@@ -446,7 +479,7 @@
 
     def cand_copy(offset):
         return pltpu.make_async_remote_copy(
-            src_ref=cand_hbm,
+            src_ref=cand_mine,
             dst_ref=cand_rows.at[my_row],
             send_sem=cand_send_sem.at[offset],
             recv_sem=cand_recv_sem.at[my_row],
@@ -454,10 +487,7 @@
             device_id_type=MESH,
         )
 
-    cand_local = pltpu.make_async_copy(cand_hbm, cand_rows.at[my_row], cand_recv_sem.at[my_row])
-    pl.when(at_home)(lambda: cand_local.start())
-    pl.when(jnp.logical_not(at_home))(lambda: cand_copy(0).start())
-    pl.loop(1, NX * NZ)(lambda offset: cand_copy(offset).start())
+    cand_local = pltpu.make_async_copy(cand_mine, cand_rows.at[my_row], cand_recv_sem.at[my_row])
     for i in (6, 7):
         loads[i].wait()
     swaps[1].wait_recv()
@@ -473,6 +503,9 @@
         return made
 
     feed_own = feed(y)
+    pl.when(at_home)(lambda: cand_local.start())
+    pl.when(jnp.logical_not(at_home))(lambda: cand_copy(0).start())
+    pl.loop(1, NX * NZ)(lambda offset: cand_copy(offset).start())
     hidden_copy(0, 0, 0).wait_recv()
     send_hidden(0, 1, 0)
     hidden_copy(1, 0, 1).wait_recv()
@@ -480,40 +513,44 @@
     hidden_copy(0, 0, 1).wait_recv()
     hidden_copy(1, 0, 0).wait_recv()
     feed_up, feed_down = feed(y_up), feed(y_down)
-    @pl.loop(0, NX * NZ)
-    def _(row):
-        pltpu.make_async_copy(cand_hbm, cand_rows.at[row], cand_recv_sem.at[row]).wait()
-
-    lane = lax.broadcasted_iota(jnp.int32, (NX * NZ, 128), 1)
-    named = cand_rows[...].reshape(NX * NZ, 128)
-    mine = jnp.logical_and(lax.shift_right_logical(named, 6) == doc, lane < 96)
-    mine_f = jnp.where(mine, 1.0, 0.0)
-    before = (
-        lax.broadcasted_iota(jnp.int32, (128, 128), 0) < lax.broadcasted_iota(jnp.int32, (128, 128), 1)
-    ).astype(F32).astype(BF16)
-    rank = jnp.dot(mine_f.astype(BF16), before, preferred_element_type=F32)
-    rows_table = jnp.zeros((NX * NZ, 128), jnp.int32)
-    places = []
-    for slot in range(SLOTS):
-        chosen = jnp.where(rank == float(slot), mine_f, 0.0)
-        some = jnp.sum(chosen, axis=1, keepdims=True)
-        place = jnp.sum(chosen * lane.astype(F32), axis=1, keepdims=True).astype(jnp.int32)
-        which = jnp.sum(
-            chosen * lax.bitwise_and(named, DOC_DEV - 1).astype(F32), axis=1, keepdims=True
-        ).astype(jnp.int32)
-        places.append(jnp.where(some > 0.5, place, 127))
-        rows_table = jnp.where(lane == slot, lax.shift_right_logical(place, 3) * 2, rows_table)
-        rows_table = jnp.where(lane == slot + 8, which, rows_table)
-    table[...] = rows_table
-    table_copy = pltpu.make_async_copy(table, table_smem, table_sem.at[0])
-    table_copy.start()
     hidden_copy(0, 1, 0).wait_recv()
     hidden_copy(1, 1, 1).wait_recv()
+    lane = lax.broadcasted_iota(jnp.int32, (NX * NZ, 128), 1)
+    places = []
+    table_copy = pltpu.make_async_copy(table, table_smem, table_sem.at[0])
+
+    def slots_then_own():
+        @pl.loop(0, NX * NZ)
+        def _(row):
+            pltpu.make_async_copy(cand_mine, cand_rows.at[row], cand_recv_sem.at[row]).wait()
+
+        named = cand_rows[...].reshape(NX * NZ, 128)
+        mine = jnp.logical_and(lax.shift_right_logical(named, 6) == doc, lax.bitwise_and(lane, 15) < 12)
+        mine_f = jnp.where(mine, 1.0, 0.0)
+        before = (
+            lax.broadcasted_iota(jnp.int32, (128, 128), 0) < lax.broadcasted_iota(jnp.int32, (128, 128), 1)
+        ).astype(F32).astype(BF16)
+        rank = jnp.dot(mine_f.astype(BF16), before, preferred_element_type=F32)
+        rows_table = jnp.zeros((NX * NZ, 128), jnp.int32)
+        for slot in range(SLOTS):
+            chosen = jnp.where(rank == float(slot), mine_f, 0.0)
+            some = jnp.sum(chosen, axis=1, keepdims=True)
+            place = jnp.sum(chosen * lane.astype(F32), axis=1, keepdims=True).astype(jnp.int32)
+            which = jnp.sum(
+                chosen * lax.bitwise_and(named, DOC_DEV - 1).astype(F32), axis=1, keepdims=True
+            ).astype(jnp.int32)
+            places.append(jnp.where(some > 0.5, place, 127))
+            rows_table = jnp.where(lane == slot, lax.bitwise_and(place, 15) * 2, rows_table)
+            rows_table = jnp.where(lane == slot + 8, which, rows_table)
+        table[...] = rows_table
+        table_copy.start()
+        return feed_own
+
     total_two, sent_three = reduce_rows(
-        1, lambda: feed(y_far), lambda: feed_up, lambda: feed_down, lambda: feed_own
+        1, lambda: feed(y_far), lambda: feed_up, lambda: feed_down, slots_then_own
     )
-    two = norm_rows(one.astype(F32) + total_two, gain_two_ref[...]).astype(BF16)
-    projected = jnp.dot(two, w_proj_ref[...], preferred_element_type=F32)
+    two = norm_rows(one.astype(F32) + total_two, gains[8:9, :]).astype(BF16)
+    projected = jnp.dot(two, w_proj[...], preferred_element_type=F32)
     unit = projected * lax.rsqrt(jnp.sum(projected * projected, axis=-1, keepdims=True) + 1e-06)
     vectors[head] = unit.astype(BF16).reshape(3, 16, 128)
 
@@ -588,9 +625,13 @@
         shared[-1].start()
     for copy in sent_four:
         copy.wait_recv()
+    outs = []
     for block in range(2 * NY):
-        place = (block % 2) * half + (block // 2) * part
-        query_out[place : place + part, :] = vectors[block].reshape(part, 128)
+        place = (block % 2) * 12 + (block // 2) * 3
+        outs.append(
+            pltpu.make_async_copy(vectors.at[block], query_out.at[pl.ds(place, 3)], load_sem.at[block])
+        )
+        outs[-1].start()
     for offset in (1, 3, 2):
         for half_index in range(2):
             index = mod(x - offset, NX) * 2 + half_index
@@ -607,10 +648,10 @@
     row_index = lax.broadcasted_iota(jnp.int32, (256, 2 * QLEN), 0)
     first_lanes = lax.broadcasted_iota(jnp.int32, (1, 2 * QLEN), 1) < QLEN
 
-    @pl.loop(0, NX * NZ)
-    def _(row):
-        source = lax.div(row, NY)
-        for pair in range(SLOTS // 2):
+    @pl.loop(0, NX * NZ // ROWS)
+    def _(step):
+        source = lax.div(step * ROWS, NY)
+        for row, pair in [(step * ROWS + i, pair) for i in range(ROWS) for pair in range(SLOTS // 2)]:
             found = []
             for slot in (2 * pair, 2 * pair + 1):
                 which = jnp.clip(table_smem[row, slot + 8], 0, DOC_DEV - 1)
@@ -673,7 +714,16 @@
     def _(row):
         pltpu.make_async_copy(back_send.at[0], back_recv.at[row], back_recv_sem.at[row]).wait()
 
-    score_out[...] = jnp.sum(back_recv[...], axis=0)
+    answer = jnp.broadcast_to(jnp.sum(back_recv[...], axis=0), (8, 128))
+    spot = lax.broadcasted_iota(jnp.int32, (8, 128), 0)
+    turned = answer
+    for i in range(1, 8):
+        turned = jnp.where(spot == i, pltpu.roll(answer, 128 - 16 * i, 1), turned)
+    score_tile[...] = turned[:, : score_tile.shape[1]]
+    outs.append(pltpu.make_async_copy(score_tile, score_out, load_sem.at[8]))
+    outs[-1].start()
+    for copy in outs:
+        copy.wait()
 
     @pl.loop(0, NX * NZ)
     def _(row):
@@ -694,18 +744,27 @@
     half = rows // 2
     part = half // NY
     anywhere = pl.BlockSpec(memory_space=pl.ANY)
-    vmem = pl.BlockSpec(memory_space=pltpu.VMEM)
-    smem = pl.BlockSpec(memory_space=pltpu.SMEM)
     dma = pltpu.SemaphoreType.DMA
     return pl.pallas_call(
         functools.partial(encoder_kernel, plan),
-        out_shape=(jax.ShapeDtypeStruct((rows, 128), BF16), jax.ShapeDtypeStruct((1, 128), F32)),
-        in_specs=[smem] + [anywhere] * 5 + [vmem, vmem, anywhere, anywhere, vmem, anywhere, smem, anywhere],
-        out_specs=(vmem, vmem),
+        out_shape=(
+            jax.ShapeDtypeStruct((rows // 16, 16, 128), BF16),
+            jax.ShapeDtypeStruct(named.shape, F32),
+        ),
+        in_specs=[anywhere] * 14,
+        out_specs=(anywhere, anywhere),
         scratch_shapes=[
+            pltpu.SMEM(group_ids.shape, jnp.int32),
+            pltpu.VMEM((16, width), F32),
+            pltpu.VMEM((width, 128), BF16),
+            pltpu.SMEM(lengths.shape, jnp.int32),
+            pltpu.VMEM(named.shape, jnp.int32),
+            pltpu.VMEM((8, 128), jnp.int32),
+            pltpu.VMEM((1, 128), jnp.int32),
+            pltpu.VMEM(named.shape, F32),
             pltpu.VMEM((2, 64, PLEN, 128), BF16),
             pltpu.VMEM((rows, width), BF16),
-            pltpu.VMEM((width, 384), BF16),
+            pltpu.VMEM((3, width, 128), BF16),
             pltpu.VMEM((2, 128, width), BF16),
             pltpu.VMEM((2, width, 512), BF16),
             pltpu.VMEM((2, 512, width), BF16),
@@ -723,7 +782,7 @@
             pltpu.VMEM((2, 2, 2, part, 512), BF16),
             pltpu.VMEM((NY, 2, part, 512), BF16),
             pltpu.VMEM((2 * NY, 3, 16, 128), BF16),
-            dma((9,)),
+            dma((15,)),
             dma((len(plan),)),
             dma((len(plan),)),
             dma((3,)),
@@ -762,7 +821,7 @@
     )(
         group_ids,
         tokens,
-        w_qkv.reshape(width, 384),
+        jnp.transpose(w_qkv, (1, 0, 2)),
         w_out,
         w_up,
         w_down,
@@ -793,7 +852,6 @@
     group_ids,
     candidates,
 ):
-    named = jnp.pad(candidates.reshape(1, -1), ((0, 0), (0, 128 - candidates.size)), constant_values=-1)
     query_vectors, rated = encode(
         tokens,
         w_qkv,
@@ -807,10 +865,10 @@
         w_proj,
         doc_vectors,
         doc_lengths,
-        named,
+        candidates.T,
         group_ids,
     )
-    return (query_vectors, rated[0, : candidates.size].reshape(candidates.shape))
+    return (query_vectors.reshape(tokens.shape[0], 128), rated.T)
 
 
 def solution(mesh):

time: 102 us -> 87.8 us (0.86)
  Pallas kernels: 93.6 us -> 83.4 us
  local copies, waits for them, and re-layouts: 6.84 us -> 2.81 us
    pallas_call x1, Pallas kernels: 93.6 us -> 83.4 us  [encode(): pl.pallas_call(functools.partial(encoder_kernel, plan), out_shape=(jax.Sh...]
    unnamed x4 -> x2, local copies, waits for them, and re-layouts: 4.39 us -> 2.81 us
    reshape x2 -> x0, local copies, waits for them, and re-layouts: 1.23 us -> none  [the longest x1 1.15 us: encode(): w_qkv.reshape(width, 384)]
where the time goes in v3:
time: 87.8 us; the launch traced here: 86.8 us
  Pallas kernels  83.4 us (95%)
  local copies, waits for them, and re-layouts  2.81 us (3%)
    pallas_call x1, Pallas kernels, encode(): pl.pallas_call(functools.partial(encoder_kernel, plan), out_shape=(jax.Sh...  83.4 us
    unnamed x2, local copies, waits for them, and re-layouts  2.81 us

profile of v3, /device:TPU:1, one launch (start us, length us, event | category | flops | bytes accessed | tf_op | source)
XLA Modules:
  0.0 86.8 jit_solution(17090957798736739186)
XLA Ops:
  0.6 83.4 %encoder.1 = (bf16[24,16,128]{2,1,0:T(8,128)(2,1)}, f32[8,12]{1,0:T(8,128)}) custom-call(s32[12]{0:T(128)} %group_hbm.1, bf16[384,1024]{1,0:T(8,128)(2,1)} %tokens_hbm.1, bf16[3,1024,128]{2,1,0:T(8,128)(2,1)} %bitcast.7, bf16[128,1024]{1,0:T(8,128)(2,1)} %w_out_hbm.1, bf16[1024,512]{1,0:T(8,128)(2,1)} %w_up_hbm.1, bf16[512,1024]{1,0:T(8,128)(2,1)} %w_down_hbm.1, ...), custom_call_target="tpu_custom_call" | custom-call | tf_op jit(solution)/shard_map/encoder/pallas_call | solution.py:748
  84.0 1.5 %copy.18 = bf16[384,128]{1,0:T(8,128)(2,1)} copy(bf16[384,128]{1,0:T(8,128)(2,1)} %bitcast.8) | data formatting | bytes 196608
  85.5 1.3 %copy.19 = f32[12,8]{0,1:T(8,128)} copy(f32[12,8]{0,1:T(8,128)} %bitcast.13) | data formatting | bytes 768

commit v4 on v3

--- a/solution.py
+++ b/solution.py
@@ -173,6 +173,7 @@
     vec_recv_sem,
     docs,
     queries,
+    near_queries,
     cand_rows,
     table,
     table_smem,
@@ -516,7 +517,6 @@
     hidden_copy(0, 1, 0).wait_recv()
     hidden_copy(1, 1, 1).wait_recv()
     lane = lax.broadcasted_iota(jnp.int32, (NX * NZ, 128), 1)
-    places = []
     table_copy = pltpu.make_async_copy(table, table_smem, table_sem.at[0])
 
     def slots_then_own():
@@ -539,7 +539,7 @@
             which = jnp.sum(
                 chosen * lax.bitwise_and(named, DOC_DEV - 1).astype(F32), axis=1, keepdims=True
             ).astype(jnp.int32)
-            places.append(jnp.where(some > 0.5, place, 127))
+            rows_table = jnp.where(lane == slot + 16, jnp.where(some > 0.5, place, 127), rows_table)
             rows_table = jnp.where(lane == slot, lax.bitwise_and(place, 15) * 2, rows_table)
             rows_table = jnp.where(lane == slot + 8, which, rows_table)
         table[...] = rows_table
@@ -554,6 +554,49 @@
     unit = projected * lax.rsqrt(jnp.sum(projected * projected, axis=-1, keepdims=True) + 1e-06)
     vectors[head] = unit.astype(BF16).reshape(3, 16, 128)
 
+    half_doc = lax.div(z, 4)
+    piece_rows = pl.ds(core * 12 + y * 3, 3)
+
+    def spread_copy(offset):
+        return pltpu.make_async_remote_copy(
+            src_ref=vectors.at[head],
+            dst_ref=near_queries.at[half_doc, piece_rows],
+            send_sem=spread_send_sem.at[offset],
+            recv_sem=spread_recv_sem.at[half_doc, y],
+            device_id=(2 * home + core, x * NZ + mod(z + offset, NZ)),
+            device_id_type=MESH,
+        )
+
+    def across_copy(half_index, source_y, offset, index):
+        rows = pl.ds(core * 12 + source_y * 3, 3)
+        return pltpu.make_async_remote_copy(
+            src_ref=near_queries.at[half_index, rows],
+            dst_ref=queries.at[index, rows],
+            send_sem=across_send_sem.at[half_index, source_y, offset - 1],
+            recv_sem=across_recv_sem.at[half_index, source_y, offset - 1],
+            device_id=(head, mod(x + offset, NX) * NZ + z),
+            device_id_type=MESH,
+        )
+
+    def share_copy(place, index):
+        held = near_queries.at[place] if place < 2 else queries.at[index]
+        rows = held.at[pl.ds(core * 12, 12)]
+        return pltpu.make_async_remote_copy(
+            src_ref=rows,
+            dst_ref=rows,
+            send_sem=share_send_sem.at[place],
+            recv_sem=share_recv_sem.at[place],
+            device_id=partner,
+            device_id_type=MESH,
+        )
+
+    spread_local = pltpu.make_async_copy(
+        vectors.at[head], near_queries.at[half_doc, piece_rows], spread_recv_sem.at[half_doc, y]
+    )
+    pl.when(at_home)(lambda: spread_local.start())
+    pl.when(jnp.logical_not(at_home))(lambda: spread_copy(0).start())
+    for offset in (4, 3, 5, 2, 6, 1, 7):
+        spread_copy(offset).start()
     sent_four = []
     for i, device in enumerate(peers):
         copy = pltpu.make_async_remote_copy(
@@ -566,60 +609,29 @@
         )
         copy.start()
         sent_four.append(copy)
-    half_doc = lax.div(z, 4)
-    piece_rows = pl.ds(core * 12 + y * 3, 3)
-
-    def spread_copy(offset):
-        return pltpu.make_async_remote_copy(
-            src_ref=vectors.at[head],
-            dst_ref=queries.at[x * 2 + half_doc, piece_rows],
-            send_sem=spread_send_sem.at[offset],
-            recv_sem=spread_recv_sem.at[half_doc, y],
-            device_id=(2 * home + core, x * NZ + mod(z + offset, NZ)),
-            device_id_type=MESH,
-        )
-
-    def across_copy(half_index, source_y, offset, index):
-        rows = queries.at[index, pl.ds(core * 12 + source_y * 3, 3)]
-        return pltpu.make_async_remote_copy(
-            src_ref=rows,
-            dst_ref=rows,
-            send_sem=across_send_sem.at[half_index, source_y, offset - 1],
-            recv_sem=across_recv_sem.at[half_index, source_y, offset - 1],
-            device_id=(head, mod(x + offset, NX) * NZ + z),
-            device_id_type=MESH,
-        )
-
-    def share_copy(place, index):
-        rows = queries.at[index, pl.ds(core * 12, 12)]
-        return pltpu.make_async_remote_copy(
-            src_ref=rows,
-            dst_ref=rows,
-            send_sem=share_send_sem.at[place],
-            recv_sem=share_recv_sem.at[place],
-            device_id=partner,
-            device_id_type=MESH,
-        )
-
-    spread_local = pltpu.make_async_copy(
-        vectors.at[head], queries.at[x * 2 + half_doc, piece_rows], spread_recv_sem.at[half_doc, y]
-    )
-    pl.when(at_home)(lambda: spread_local.start())
-    pl.when(jnp.logical_not(at_home))(lambda: spread_copy(0).start())
-    for offset in (4, 3, 5, 2, 6, 1, 7):
-        spread_copy(offset).start()
     crossing = []
     shared = []
-    for source_y in range(NY):
-        for half_index in range(2):
-            pltpu.make_async_copy(
-                vectors.at[head],
-                queries.at[x * 2 + half_index, pl.ds(core * 12 + source_y * 3, 3)],
-                spread_recv_sem.at[half_index, source_y],
-            ).wait()
-            for offset in (2, 1, 3):
-                crossing.append(across_copy(half_index, source_y, offset, x * 2 + half_index))
-                crossing[-1].start()
+    ahead = mod(mod(y - x, NY) - z, NZ)
+    near = jnp.where(jnp.logical_or(ahead <= 2, ahead >= 6), 0, 1)
+    for step, half_index in (
+        (0, near),
+        (1, near),
+        (3, near),
+        (0, 1 - near),
+        (2, near),
+        (1, 1 - near),
+        (3, 1 - near),
+        (2, 1 - near),
+    ):
+        source_y = mod(y + step, NY)
+        pltpu.make_async_copy(
+            vectors.at[head],
+            near_queries.at[half_index, pl.ds(core * 12 + source_y * 3, 3)],
+            spread_recv_sem.at[half_index, source_y],
+        ).wait()
+        for offset in (2, 1, 3):
+            crossing.append(across_copy(half_index, source_y, offset, x * 2 + half_index))
+            crossing[-1].start()
     for half_index in range(2):
         shared.append(share_copy(half_index, x * 2 + half_index))
         shared[-1].start()
@@ -632,53 +644,13 @@
             pltpu.make_async_copy(vectors.at[block], query_out.at[pl.ds(place, 3)], load_sem.at[block])
         )
         outs[-1].start()
-    for offset in (1, 3, 2):
-        for half_index in range(2):
-            index = mod(x - offset, NX) * 2 + half_index
-            for source_y in range(NY):
-                across_copy(half_index, source_y, offset, index).wait_recv()
-            shared.append(share_copy(2 * offset + half_index, index))
-            shared[-1].start()
     table_copy.wait()
     loads[8].wait()
-    for copy in shared:
-        copy.wait_recv()
 
     zeros = jnp.zeros((QLEN, 128), BF16)
     row_index = lax.broadcasted_iota(jnp.int32, (256, 2 * QLEN), 0)
     first_lanes = lax.broadcasted_iota(jnp.int32, (1, 2 * QLEN), 1) < QLEN
-
-    @pl.loop(0, NX * NZ // ROWS)
-    def _(step):
-        source = lax.div(step * ROWS, NY)
-        for row, pair in [(step * ROWS + i, pair) for i in range(ROWS) for pair in range(SLOTS // 2)]:
-            found = []
-            for slot in (2 * pair, 2 * pair + 1):
-                which = jnp.clip(table_smem[row, slot + 8], 0, DOC_DEV - 1)
-                request = jnp.clip(table_smem[row, slot], 0, 22)
-                query = jnp.concatenate([queries[source, request], queries[source, request + 1]], axis=0)
-                found.append((docs[which], query, lengths_ref[which]))
-            (doc_a, query_a, len_a), (doc_b, query_b, len_b) = found
-            left = jnp.concatenate([doc_a, doc_b], axis=1)
-            right = jnp.concatenate(
-                [
-                    jnp.concatenate([query_a, zeros], axis=1),
-                    jnp.concatenate([zeros, query_b], axis=1),
-                ],
-                axis=0,
-            )
-            sims = lax.dot_general(left, right, NT, preferred_element_type=F32)
-            live = row_index < jnp.where(first_lanes, len_a, len_b)
-            best_rows[pair, pl.ds(row, 1), : 2 * QLEN] = jnp.max(
-                jnp.where(live, sims, -jnp.inf), axis=0, keepdims=True
-            )
-
-    rated = jnp.zeros((NX * NZ, 128), F32)
-    for slot in range(SLOTS):
-        low = (slot % 2) * QLEN
-        value = jnp.sum(best_rows[slot // 2][:, low : low + QLEN], axis=1, keepdims=True)
-        rated = rated + jnp.where(lane == places[slot], value, 0.0)
-    back_send[...] = rated.reshape(NX * NZ, 1, 128)
+    eight_lanes = lax.broadcasted_iota(jnp.int32, (8, 128), 1)
 
     def back_to(row):
         source_x, source_half, source_y = lax.div(row, 8), lax.rem(lax.div(row, NY), 2), lax.rem(row, NY)
@@ -700,15 +672,75 @@
         source, source_y = back_to(row)
         return jnp.logical_and(source == doc, source_y == y)
 
-    @pl.loop(0, NX * NZ)
-    def _(row):
-        own_row = is_own(row)
-        pl.when(own_row)(
-            lambda: pltpu.make_async_copy(
-                back_send.at[row], back_recv.at[doc], back_recv_sem.at[doc]
-            ).start()
-        )
-        pl.when(jnp.logical_not(own_row))(lambda: back_copy(row).start())
+    def rate(source_x, local):
+        base = source_x * 8
+
+        @pl.loop(0, 8 // ROWS)
+        def _(step):
+            first = base + step * ROWS
+            held = near_queries.at[step] if local else queries.at[lax.div(first, NY)]
+            for row, pair in [(first + i, pair) for i in range(ROWS) for pair in range(SLOTS // 2)]:
+                found = []
+                for slot in (2 * pair, 2 * pair + 1):
+                    which = jnp.clip(table_smem[row, slot + 8], 0, DOC_DEV - 1)
+                    request = jnp.clip(table_smem[row, slot], 0, 22)
+                    query = jnp.concatenate([held[request], held[request + 1]], axis=0)
+                    found.append((docs[which], query, lengths_ref[which]))
+                (doc_a, query_a, len_a), (doc_b, query_b, len_b) = found
+                left = jnp.concatenate([doc_a, doc_b], axis=1)
+                right = jnp.concatenate(
+                    [
+                        jnp.concatenate([query_a, zeros], axis=1),
+                        jnp.concatenate([zeros, query_b], axis=1),
+                    ],
+                    axis=0,
+                )
+                sims = lax.dot_general(left, right, NT, preferred_element_type=F32)
+                live = row_index < jnp.where(first_lanes, len_a, len_b)
+                best_rows[pair, pl.ds(row, 1), : 2 * QLEN] = jnp.max(
+                    jnp.where(live, sims, -jnp.inf), axis=0, keepdims=True
+                )
+
+        eight = pl.ds(pl.multiple_of(base, 8), 8)
+        spots = table[eight, :]
+        rated = jnp.zeros((8, 128), F32)
+        for slot in range(SLOTS):
+            low = (slot % 2) * QLEN
+            value = jnp.sum(best_rows[slot // 2, eight, low : low + QLEN], axis=1, keepdims=True)
+            rated = rated + jnp.where(eight_lanes == spots[:, slot + 16 : slot + 17], value, 0.0)
+        back_send[pl.ds(base, 8)] = rated.reshape(8, 1, 128)
+
+    def send_back(source_x, local):
+        for step in (2, 1, 3, 0):
+            for half_index in range(2):
+                row = source_x * 8 + half_index * NY + mod(y + step, NY)
+                if local and step == 0:
+                    own_row = is_own(row)
+                    pl.when(own_row)(
+                        lambda row=row: pltpu.make_async_copy(
+                            back_send.at[row], back_recv.at[doc], back_recv_sem.at[doc]
+                        ).start()
+                    )
+                    pl.when(jnp.logical_not(own_row))(lambda row=row: back_copy(row).start())
+                else:
+                    back_copy(row).start()
+
+    for copy in shared:
+        copy.wait_recv()
+    rate(x, True)
+    send_back(x, True)
+    for offset in (1, 3, 2):
+        for half_index in range(2):
+            index = mod(x - offset, NX) * 2 + half_index
+            for source_y in range(NY):
+                across_copy(half_index, source_y, offset, index).wait_recv()
+            shared.append(share_copy(2 * offset + half_index, index))
+            shared[-1].start()
+    for copy in shared[2:]:
+        copy.wait_recv()
+    for offset in (2, 1, 3):
+        rate(mod(x - offset, NX), False)
+        send_back(mod(x - offset, NX), False)
 
     @pl.loop(0, NX * NZ)
     def _(row):
@@ -798,6 +830,7 @@
             dma((7,)),
             pltpu.VMEM((64, 256, 128), BF16),
             pltpu.VMEM((8, 24, 16, 128), BF16),
+            pltpu.VMEM((2, 24, 16, 128), BF16),
             pltpu.VMEM((32, 1, 128), jnp.int32),
             pltpu.VMEM((32, 128), jnp.int32),
             pltpu.SMEM((32, 128), jnp.int32),

time: 87.8 us -> 86.6 us (0.986)
  no operation moved by 1% of the time
where the time goes in v4:
time: 86.6 us; the launch traced here: 86.4 us
  Pallas kernels  83 us (96%)
  local copies, waits for them, and re-layouts  2.81 us (3%)
    pallas_call x1, Pallas kernels, encode(): pl.pallas_call(functools.partial(encoder_kernel, plan), out_shape=(jax.Sh...  83 us
    unnamed x2, local copies, waits for them, and re-layouts  2.81 us

profile of v4, /device:TPU:1, one launch (start us, length us, event | category | flops | bytes accessed | tf_op | source)
XLA Modules:
  0.0 86.4 jit_solution(15638502565114542773)
XLA Ops:
  0.6 83.0 %encoder.1 = (bf16[24,16,128]{2,1,0:T(8,128)(2,1)}, f32[8,12]{1,0:T(8,128)}) custom-call(s32[12]{0:T(128)} %group_hbm.1, bf16[384,1024]{1,0:T(8,128)(2,1)} %tokens_hbm.1, bf16[3,1024,128]{2,1,0:T(8,128)(2,1)} %bitcast.7, bf16[128,1024]{1,0:T(8,128)(2,1)} %w_out_hbm.1, bf16[1024,512]{1,0:T(8,128)(2,1)} %w_up_hbm.1, bf16[512,1024]{1,0:T(8,128)(2,1)} %w_down_hbm.1, ...), custom_call_target="tpu_custom_call" | custom-call | tf_op jit(solution)/shard_map/encoder/pallas_call | solution.py:780
  83.6 1.5 %copy.18 = bf16[384,128]{1,0:T(8,128)(2,1)} copy(bf16[384,128]{1,0:T(8,128)(2,1)} %bitcast.8) | data formatting | bytes 196608
  85.1 1.3 %copy.19 = f32[12,8]{0,1:T(8,128)} copy(f32[12,8]{0,1:T(8,128)} %bitcast.13) | data formatting | bytes 768

commit v5 on v4

--- a/solution.py
+++ b/solution.py
@@ -76,7 +76,7 @@
         firsts = along_z(kv, 0, low, rows, None, True)
         along_x(kv, 0, low, rows, None, False)
         for first in firsts:
-            along_x(kv, first.dz, first.low, first.rows, first, False)
+            along_x(kv, first.dz, first.low, first.rows, first, abs(first.dz) == 4)
     for kv, low, rows in X_FIRST:
         firsts = along_x(kv, 0, low, rows, None, True)
         along_z(kv, 0, low, rows, None, False)
@@ -137,7 +137,10 @@
     cand_wide,
     cand_mine,
     score_tile,
-    cache,
+    cache_keys,
+    cache_values,
+    prob,
+    sums,
     tokens,
     w_qkv,
     w_out,
@@ -221,9 +224,7 @@
         pltpu.make_async_copy(w_qkv_hbm, w_qkv, load_sem.at[1]),
         pltpu.make_async_copy(rel_hbm.at[pl.ds(RELS // 2 - 96, 128)], rel.at[0], load_sem.at[2]),
         pltpu.make_async_copy(rel_hbm.at[pl.ds(RELS // 2 - 32, 128)], rel.at[1], load_sem.at[3]),
-        pltpu.make_async_copy(
-            cache_hbm, cache.at[:, pl.ds(doc * 2, 2)], load_sem.at[4]
-        ),
+        pltpu.make_async_copy(cache_hbm.at[0], cache_keys.at[pl.ds(doc * 2, 2)], load_sem.at[4]),
         pltpu.make_async_copy(w_out_hbm, w_out.at[core], load_sem.at[5]),
         pltpu.make_async_copy(w_up_hbm, w_up.at[core], load_sem.at[6]),
         pltpu.make_async_copy(w_down_hbm, w_down.at[core], load_sem.at[7]),
@@ -234,6 +235,7 @@
         pltpu.make_async_copy(lengths_hbm, lengths_ref, load_sem.at[12]),
         pltpu.make_async_copy(cand_hbm, cand_tile, load_sem.at[13]),
         pltpu.make_async_copy(group_hbm, group_ref, load_sem.at[14]),
+        pltpu.make_async_copy(cache_hbm.at[1], cache_values.at[pl.ds(doc * 2, 2)], load_sem.at[15]),
     ]
     for load in loads:
         load.start()
@@ -247,10 +249,11 @@
             dz -= message.sign * message.hops
         block = mod(x - dx, NX) * NZ + mod(z - dz, NZ)
         group, low = block * 2 + message.low // PLEN, message.low % PLEN
+        held = cache_values if message.kv else cache_keys
         if message.rows == 2 * PLEN:
-            target = cache.at[message.kv, pl.ds(group, 2)]
+            target = held.at[pl.ds(group, 2)]
         else:
-            target = cache.at[message.kv, group, pl.ds(low, message.rows)]
+            target = held.at[group, pl.ds(low, message.rows)]
         source = target
         if message.parent is None:
             source = cache_hbm.at[message.kv]
@@ -314,25 +317,28 @@
         q_all = q_mask[0, rows, :] + q_mask[1, rows, :]
         q_rel[rows, :] = lax.dot_general(q_all, rel_two[1], NT, preferred_element_type=F32)
     loads[4].wait()
-    for i in range(9, 15):
+    for i in range(9, 16):
         loads[i].wait()
     cand_wide[...] = jnp.zeros_like(cand_wide)
     cand_wide[:, : cand_tile.shape[1]] = cand_tile[...]
     cand_mine[...] = jnp.sum(pltpu.roll(cand_wide[...], 0, 1, stride=16, stride_axis=0), axis=0, keepdims=True)
 
     for message in plan:
-        copies[message.index].wait_recv()
+        if message.children:
+            copies[message.index].wait_recv()
         for child in message.children:
             copies[child.index].start()
+    for message in plan:
+        if message.kv == 0 and not message.children:
+            copies[message.index].wait_recv()
 
     low_lane = lax.broadcasted_iota(jnp.int32, (96, 128), 1) < QLEN
     low_half = lax.broadcasted_iota(jnp.int32, (QLEN, 128), 1) < HD
 
-    def attend(request):
+    def weigh(place, request):
         group = group_ref[request]
         own = pl.ds(pl.multiple_of(request * QLEN, QLEN), QLEN)
-        keys = jnp.concatenate([cache[0, group], k_own[own, :]], axis=0)
-        values = jnp.concatenate([cache[1, group], v_own[own, :]], axis=0)
+        keys = jnp.concatenate([cache_keys[group], k_own[own, :]], axis=0)
         query = jnp.concatenate([q_mask[0, own, :], q_mask[1, own, :]], axis=0)
         content = lax.dot_general(query, keys, NT, preferred_element_type=F32)
         key_rel = lax.dot_general(keys, rel_two[0], NT, preferred_element_type=F32)
@@ -350,13 +356,25 @@
         logits = (content + c2p + p2c) * (1.0 / math.sqrt(3 * HD))
         weights = jnp.exp(logits - jnp.max(logits, axis=-1, keepdims=True))
         total = jnp.sum(weights, axis=-1, keepdims=True)
-        out = jnp.dot(weights.astype(BF16), values, preferred_element_type=F32) / total
+        prob[place, :, : PLEN + QLEN] = weights.astype(BF16)
+        sums[place] = jnp.broadcast_to(total, (2 * QLEN, 128))
+
+    def blend(place, request):
+        own = pl.ds(pl.multiple_of(request * QLEN, QLEN), QLEN)
+        values = jnp.concatenate([cache_values[group_ref[request]], v_own[own, :]], axis=0)
+        out = jnp.dot(prob[place, :, : PLEN + QLEN], values, preferred_element_type=F32) / sums[place]
         return jnp.where(low_half, out[:QLEN], out[QLEN:]).astype(BF16)
 
     half = tokens.shape[0] // 2
     per_core = half // QLEN
     for i in range(per_core):
-        att_send[i * QLEN : i * QLEN + QLEN, :] = attend((1 - core) * per_core + i)
+        weigh(i, (1 - core) * per_core + i)
+        weigh(per_core + i, core * per_core + i)
+    for message in plan:
+        if message.kv == 1 and not message.children:
+            copies[message.index].wait_recv()
+    for i in range(per_core):
+        att_send[i * QLEN : i * QLEN + QLEN, :] = blend(i, (1 - core) * per_core + i)
     att_copy = pltpu.make_async_remote_copy(
         src_ref=att_send,
         dst_ref=att.at[core],
@@ -367,7 +385,7 @@
     )
     att_copy.start()
     for i in range(per_core):
-        att[core, i * QLEN : i * QLEN + QLEN, :] = attend(core * per_core + i)
+        att[core, i * QLEN : i * QLEN + QLEN, :] = blend(per_core + i, core * per_core + i)
     att_copy.wait_recv()
     loads[5].wait()
     swaps[0].wait_recv()
@@ -794,7 +812,10 @@
             pltpu.VMEM((8, 128), jnp.int32),
             pltpu.VMEM((1, 128), jnp.int32),
             pltpu.VMEM(named.shape, F32),
-            pltpu.VMEM((2, 64, PLEN, 128), BF16),
+            pltpu.VMEM((64, PLEN, 128), BF16),
+            pltpu.VMEM((64, PLEN, 128), BF16),
+            pltpu.VMEM((rows // QLEN, 2 * QLEN, 128), BF16),
+            pltpu.VMEM((rows // QLEN, 2 * QLEN, 128), F32),
             pltpu.VMEM((rows, width), BF16),
             pltpu.VMEM((3, width, 128), BF16),
             pltpu.VMEM((2, 128, width), BF16),
@@ -814,7 +835,7 @@
             pltpu.VMEM((2, 2, 2, part, 512), BF16),
             pltpu.VMEM((NY, 2, part, 512), BF16),
             pltpu.VMEM((2 * NY, 3, 16, 128), BF16),
-            dma((15,)),
+            dma((16,)),
             dma((len(plan),)),
             dma((len(plan),)),
             dma((3,)),

time: 86.6 us -> 84.6 us (0.977)
  Pallas kernels: 83 us -> 81 us
    pallas_call x1, Pallas kernels: 83 us -> 81 us  [encode(): pl.pallas_call(functools.partial(encoder_kernel, plan), out_shape=(jax.Sh...]
where the time goes in v5:
time: 84.6 us; the launch traced here: 84.5 us
  Pallas kernels  81 us (96%)
  local copies, waits for them, and re-layouts  2.81 us (3%)
    pallas_call x1, Pallas kernels, encode(): pl.pallas_call(functools.partial(encoder_kernel, plan), out_shape=(jax.Sh...  81 us
    unnamed x2, local copies, waits for them, and re-layouts  2.81 us

profile of v5, /device:TPU:1, one launch (start us, length us, event | category | flops | bytes accessed | tf_op | source)
XLA Modules:
  0.0 84.5 jit_solution(10480709083229461688)
XLA Ops:
  0.6 81.0 %encoder.1 = (bf16[24,16,128]{2,1,0:T(8,128)(2,1)}, f32[8,12]{1,0:T(8,128)}) custom-call(s32[12]{0:T(128)} %group_hbm.1, bf16[384,1024]{1,0:T(8,128)(2,1)} %tokens_hbm.1, bf16[3,1024,128]{2,1,0:T(8,128)(2,1)} %bitcast.7, bf16[128,1024]{1,0:T(8,128)(2,1)} %w_out_hbm.1, bf16[1024,512]{1,0:T(8,128)(2,1)} %w_up_hbm.1, bf16[512,1024]{1,0:T(8,128)(2,1)} %w_down_hbm.1, ...), custom_call_target="tpu_custom_call" | custom-call | tf_op jit(solution)/shard_map/encoder/pallas_call | solution.py:798
  81.7 1.5 %copy.18 = bf16[384,128]{1,0:T(8,128)(2,1)} copy(bf16[384,128]{1,0:T(8,128)(2,1)} %bitcast.8) | data formatting | bytes 196608
  83.2 1.3 %copy.19 = f32[12,8]{0,1:T(8,128)} copy(f32[12,8]{0,1:T(8,128)} %bitcast.13) | data formatting | bytes 768

commit v6 on v5

--- a/solution.py
+++ b/solution.py
@@ -17,7 +17,6 @@
 NZ = 8
 NY = 4
 SLOTS = 6
-ROWS = 4
 MESH = pl.DeviceIdType.MESH
 F32 = jnp.float32
 BF16 = jnp.bfloat16
@@ -693,31 +692,29 @@
     def rate(source_x, local):
         base = source_x * 8
 
-        @pl.loop(0, 8 // ROWS)
-        def _(step):
-            first = base + step * ROWS
-            held = near_queries.at[step] if local else queries.at[lax.div(first, NY)]
-            for row, pair in [(first + i, pair) for i in range(ROWS) for pair in range(SLOTS // 2)]:
-                found = []
-                for slot in (2 * pair, 2 * pair + 1):
-                    which = jnp.clip(table_smem[row, slot + 8], 0, DOC_DEV - 1)
-                    request = jnp.clip(table_smem[row, slot], 0, 22)
-                    query = jnp.concatenate([held[request], held[request + 1]], axis=0)
-                    found.append((docs[which], query, lengths_ref[which]))
-                (doc_a, query_a, len_a), (doc_b, query_b, len_b) = found
-                left = jnp.concatenate([doc_a, doc_b], axis=1)
-                right = jnp.concatenate(
-                    [
-                        jnp.concatenate([query_a, zeros], axis=1),
-                        jnp.concatenate([zeros, query_b], axis=1),
-                    ],
-                    axis=0,
-                )
-                sims = lax.dot_general(left, right, NT, preferred_element_type=F32)
-                live = row_index < jnp.where(first_lanes, len_a, len_b)
-                best_rows[pair, pl.ds(row, 1), : 2 * QLEN] = jnp.max(
-                    jnp.where(live, sims, -jnp.inf), axis=0, keepdims=True
-                )
+        for i, pair in [(i, pair) for i in range(8) for pair in range(SLOTS // 2)]:
+            row = base + i
+            held = near_queries.at[i // NY] if local else queries.at[source_x * 2 + i // NY]
+            found = []
+            for slot in (2 * pair, 2 * pair + 1):
+                which = jnp.clip(table_smem[row, slot + 8], 0, DOC_DEV - 1)
+                request = jnp.clip(table_smem[row, slot], 0, 22)
+                query = jnp.concatenate([held[request], held[request + 1]], axis=0)
+                found.append((docs[which], query, lengths_ref[which]))
+            (doc_a, query_a, len_a), (doc_b, query_b, len_b) = found
+            left = jnp.concatenate([doc_a, doc_b], axis=1)
+            right = jnp.concatenate(
+                [
+                    jnp.concatenate([query_a, zeros], axis=1),
+                    jnp.concatenate([zeros, query_b], axis=1),
+                ],
+                axis=0,
+            )
+            sims = lax.dot_general(left, right, NT, preferred_element_type=F32)
+            live = row_index < jnp.where(first_lanes, len_a, len_b)
+            best_rows[pair, pl.ds(row, 1), : 2 * QLEN] = jnp.max(
+                jnp.where(live, sims, -jnp.inf), axis=0, keepdims=True
+            )
 
         eight = pl.ds(pl.multiple_of(base, 8), 8)
         spots = table[eight, :]

time: 84.6 us -> 84.1 us (level)
  no operation moved by 1% of the time
where the time goes in v6:
time: 84.1 us; the launch traced here: 83.9 us
  Pallas kernels  80.5 us (96%)
  local copies, waits for them, and re-layouts  2.81 us (3%)
    pallas_call x1, Pallas kernels, encode(): pl.pallas_call(functools.partial(encoder_kernel, plan), out_shape=(jax.Sh...  80.5 us
    unnamed x2, local copies, waits for them, and re-layouts  2.81 us

profile of v6, /device:TPU:1, one launch (start us, length us, event | category | flops | bytes accessed | tf_op | source)
XLA Modules:
  0.0 83.9 jit_solution(10868765382510694759)
XLA Ops:
  0.6 80.5 %encoder.1 = (bf16[24,16,128]{2,1,0:T(8,128)(2,1)}, f32[8,12]{1,0:T(8,128)}) custom-call(s32[12]{0:T(128)} %group_hbm.1, bf16[384,1024]{1,0:T(8,128)(2,1)} %tokens_hbm.1, bf16[3,1024,128]{2,1,0:T(8,128)(2,1)} %bitcast.7, bf16[128,1024]{1,0:T(8,128)(2,1)} %w_out_hbm.1, bf16[1024,512]{1,0:T(8,128)(2,1)} %w_up_hbm.1, bf16[512,1024]{1,0:T(8,128)(2,1)} %w_down_hbm.1, ...), custom_call_target="tpu_custom_call" | custom-call | tf_op jit(solution)/shard_map/encoder/pallas_call | solution.py:795
  81.1 1.5 %copy.18 = bf16[384,128]{1,0:T(8,128)(2,1)} copy(bf16[384,128]{1,0:T(8,128)(2,1)} %bitcast.8) | data formatting | bytes 196608
  82.6 1.3 %copy.19 = f32[12,8]{0,1:T(8,128)} copy(f32[12,8]{0,1:T(8,128)} %bitcast.13) | data formatting | bytes 768

commit v7 on v6

--- a/solution.py
+++ b/solution.py
@@ -757,6 +757,17 @@
         rate(mod(x - offset, NX), False)
         send_back(mod(x - offset, NX), False)
 
+    pl.when(jnp.logical_not(at_home))(lambda: cand_copy(0).wait_send())
+    pl.loop(1, NX * NZ)(lambda offset: cand_copy(offset).wait_send())
+    pl.when(jnp.logical_not(at_home))(lambda: spread_copy(0).wait_send())
+    for offset in range(1, NZ):
+        spread_copy(offset).wait_send()
+    for copy in list(copies.values()) + swaps + [att_copy] + sent_one + sent_two + sent_three + sent_four + crossing + shared:
+        copy.wait_send()
+
+    for copy in outs:
+        copy.wait()
+
     @pl.loop(0, NX * NZ)
     def _(row):
         pltpu.make_async_copy(back_send.at[0], back_recv.at[row], back_recv_sem.at[row]).wait()
@@ -769,20 +780,11 @@
     score_tile[...] = turned[:, : score_tile.shape[1]]
     outs.append(pltpu.make_async_copy(score_tile, score_out, load_sem.at[8]))
     outs[-1].start()
-    for copy in outs:
-        copy.wait()
 
     @pl.loop(0, NX * NZ)
     def _(row):
         pl.when(jnp.logical_not(is_own(row)))(lambda: back_copy(row).wait_send())
-
-    pl.when(jnp.logical_not(at_home))(lambda: cand_copy(0).wait_send())
-    pl.loop(1, NX * NZ)(lambda offset: cand_copy(offset).wait_send())
-    pl.when(jnp.logical_not(at_home))(lambda: spread_copy(0).wait_send())
-    for offset in range(1, NZ):
-        spread_copy(offset).wait_send()
-    for copy in list(copies.values()) + swaps + [att_copy] + sent_one + sent_two + sent_three + sent_four + crossing + shared:
-        copy.wait_send()
+    outs[-1].wait()
 
 
 def encode(tokens, w_qkv, w_out, w_up, w_down, gain_one, gain_two, rel_table, prompt_cache, w_proj, docs, lengths, named, group_ids):

time: 84.1 us -> 83.2 us (0.989)
  Pallas kernels: 80.5 us -> 79.6 us
where the time goes in v7:
time: 83.2 us; the launch traced here: 83.1 us
  Pallas kernels  79.6 us (96%)
  local copies, waits for them, and re-layouts  2.81 us (3%)
    pallas_call x1, Pallas kernels, encode(): pl.pallas_call(functools.partial(encoder_kernel, plan), out_shape=(jax.Sh...  79.6 us
    unnamed x2, local copies, waits for them, and re-layouts  2.81 us

profile of v7, /device:TPU:1, one launch (start us, length us, event | category | flops | bytes accessed | tf_op | source)
XLA Modules:
  0.0 83.1 jit_solution(17036236983889808798)
XLA Ops:
  0.6 79.6 %encoder.1 = (bf16[24,16,128]{2,1,0:T(8,128)(2,1)}, f32[8,12]{1,0:T(8,128)}) custom-call(s32[12]{0:T(128)} %group_hbm.1, bf16[384,1024]{1,0:T(8,128)(2,1)} %tokens_hbm.1, bf16[3,1024,128]{2,1,0:T(8,128)(2,1)} %bitcast.7, bf16[128,1024]{1,0:T(8,128)(2,1)} %w_out_hbm.1, bf16[1024,512]{1,0:T(8,128)(2,1)} %w_up_hbm.1, bf16[512,1024]{1,0:T(8,128)(2,1)} %w_down_hbm.1, ...), custom_call_target="tpu_custom_call" | custom-call | tf_op jit(solution)/shard_map/encoder/pallas_call | solution.py:797
  80.3 1.5 %copy.18 = bf16[384,128]{1,0:T(8,128)(2,1)} copy(bf16[384,128]{1,0:T(8,128)(2,1)} %bitcast.8) | data formatting | bytes 196608
  81.8 1.3 %copy.19 = f32[12,8]{0,1:T(8,128)} copy(f32[12,8]{0,1:T(8,128)} %bitcast.13) | data formatting | bytes 768
